TPU v7x, 256 devices: a whole 4x4x8 slice. The times are simulated.
256 devices in a mesh: gz: 8 (over x, core), gx: 32 (over z, y).
Axes of the slice: x: 4, y: 4, z: 8, core: 2. Of those that a mesh axis runs over, the one named last changes fastest.
Arguments:
- volume: float32 [256, 512, 256], P('gz', 'gx')
- measured: float32 [2, 256, 2048], P(None, 'gz')
- weight_blocks: bfloat16 [64, 128, 128], replicated, may hold values from 0 to 2
- view_order: int32 [2], replicated, may hold values from 0 to 1, each once
- tile_voxel: int32 [2, 8, 16384], P(None, 'gz', 'gx'), may hold values from 0 to 1023
- tile_column: int32 [2, 8, 16384], P(None, 'gz', 'gx'), may hold values from 0 to 15
- tile_block: int32 [2, 8, 16384], P(None, 'gz', 'gx'), may hold values from 0 to 63
- entry_count: int32 [2, 8, 32], P(None, 'gz', 'gx'), may hold values from 1 to 512, as said below
Outputs:
- volume_out: float32 [256, 512, 256], P('gz', 'gx')
Inputs may be any that keep to these rules, and one draw needn't show every extreme that they name: Entries of block (a, c) of view v at or past entry_count[v, a, c] are not used; in every view some block has 512 live entries.
All inputs are finite; a program needn't handle non-finite values.
Results may differ from a plain program's by a relative error of at most 0.0027.
Values may be sent and summed in bfloat16 or wider, within the bound.
A program may use at most 64 MiB of HBM per device.

v0:
```python
import jax
import jax.numpy as jnp
from jax import lax
from jax.sharding import PartitionSpec as P

TV_STEPS = 4


smooth_floor = 0.01
step_gain = 0.25
norm_floor = 1e-06
group_rows = 128


def padded_2(cells, sides, width):
    for axis, dim in sides:
        count = lax.axis_size(axis)
        ends = count - 1
        head = lax.slice_in_dim(cells, 0, width, axis=dim)
        tail = lax.slice_in_dim(cells, cells.shape[dim] - width, cells.shape[dim], axis=dim)
        cells = jnp.concatenate(
            [
                lax.ppermute(tail, axis, [(i, (i + 1) % count) for i in range(ends)]),
                cells,
                lax.ppermute(head, axis, [((i + 1) % count, i) for i in range(ends)]),
            ],
            axis=dim,
        )
    return cells


def tv_grad(padded):
    base_cells = padded[:-1, :-1, :-1]
    diff_z = padded[1:, :-1, :-1] - base_cells
    diff_x = padded[:-1, 1:, :-1] - base_cells
    diff_y = padded[:-1, :-1, 1:] - base_cells
    inverse = lax.rsqrt(diff_z * diff_z + diff_x * diff_x + diff_y * diff_y + smooth_floor)
    flow_z = diff_z * inverse
    flow_x = diff_x * inverse
    flow_y = diff_y * inverse
    flow_all = flow_z + flow_x + flow_y
    return flow_z[:-1, 1:, 1:] + flow_x[1:, :-1, 1:] + flow_y[1:, 1:, :-1] - flow_all[1:, 1:, 1:]


def pad_depth(field):
    return jnp.pad(field, ((0, 0), (0, 0), (1, 1)))


def body(
    volume, measured, weight_blocks, view_order, tile_voxel, tile_column, tile_block, entry_count
):
    depth_z, depth_x, depth_y = volume.shape
    tiles_y = depth_y // group_rows
    tiles_u = measured.shape[2] // group_rows
    slab_tiles = depth_z * tiles_u
    plane_tiles = depth_x * tiles_y
    row_weight = jnp.sum(weight_blocks, axis=2, dtype=jnp.float32)
    col_weight = jnp.sum(weight_blocks, axis=1, dtype=jnp.float32)
    offsets = jnp.arange(group_rows, dtype=jnp.int32)
    current = volume
    for turn_index in range(view_order.shape[0]):
        view_index = view_order[turn_index]
        voxel_list = lax.dynamic_index_in_dim(tile_voxel, view_index, 0, keepdims=False)[0]
        column_list = lax.dynamic_index_in_dim(tile_column, view_index, 0, keepdims=False)[0]
        block_list = lax.dynamic_index_in_dim(tile_block, view_index, 0, keepdims=False)[0]
        live_count = lax.dynamic_index_in_dim(entry_count, view_index, 0, keepdims=False)[0, 0]
        rounds = (live_count + group_rows - 1) // group_rows
        voxel_tiles = current.astype(jnp.bfloat16).reshape(-1, group_rows)

        def gather_group(index):
            begin = index * group_rows
            voxels = lax.dynamic_slice_in_dim(voxel_list, begin, group_rows)
            columns = lax.dynamic_slice_in_dim(column_list, begin, group_rows)
            chosen = lax.dynamic_slice_in_dim(block_list, begin, group_rows)
            weight = (begin + offsets < live_count).astype(jnp.float32)[:, None]
            detector = voxels // plane_tiles * tiles_u + columns
            return (voxels, detector, chosen, weight)

        def forward(index, carry):
            projection, ray_sum = carry
            voxels, detector, chosen, weight = gather_group(index)
            product = jnp.einsum(
                "ejk,ek->ej",
                weight_blocks[chosen],
                voxel_tiles[voxels],
                preferred_element_type=jnp.float32,
            )
            return (
                projection.at[detector].add(product * weight),
                ray_sum.at[detector].add(row_weight[chosen] * weight),
            )

        empty = jnp.zeros((slab_tiles, group_rows), jnp.float32)
        projection, ray_sum = lax.fori_loop(0, rounds, forward, (empty, empty))
        target = lax.dynamic_index_in_dim(measured, view_index, 0, keepdims=False).reshape(
            slab_tiles, group_rows
        )
        projection, ray_sum = (
            lax.psum(projection.astype(jnp.bfloat16), "gx").astype(jnp.float32),
            lax.psum(ray_sum.astype(jnp.bfloat16), "gx").astype(jnp.float32),
        )
        residual = ((target - projection) / (ray_sum + 1.0)).astype(jnp.bfloat16)

        def backward(index, carry):
            change, voxel_sum = carry
            voxels, detector, chosen, weight = gather_group(index)
            product = jnp.einsum(
                "ejk,ej->ek",
                weight_blocks[chosen],
                residual[detector],
                preferred_element_type=jnp.float32,
            )
            return (
                change.at[voxels].add(product * weight),
                voxel_sum.at[voxels].add(col_weight[chosen] * weight),
            )

        blank = jnp.zeros((voxel_tiles.shape[0], group_rows), jnp.float32)
        change, voxel_sum = lax.fori_loop(0, rounds, backward, (blank, blank))
        current = current + (change / (voxel_sum + 1.0)).reshape(current.shape)
    art_volume = jnp.maximum(current, 0.0)
    difference = art_volume - volume
    change_part = jnp.sum(difference * difference)
    change_total = None
    change_total = lax.psum(change_part, ("gz", "gx"))
    smooth = art_volume
    for sweep_index in range(TV_STEPS):
        padded = padded_2(smooth, (("gz", 0), ("gx", 1)), 1)
        slope = tv_grad(pad_depth(padded))
        slope_part = jnp.sum(slope * slope)
        if sweep_index == 0:
            slope_total = lax.psum(slope_part, ("gz", "gx"))
        else:
            slope_total = lax.psum(slope_part, ("gz", "gx"))
        change_total, scale_now = (
            change_total,
            step_gain * jnp.sqrt(change_total) / jnp.sqrt(slope_total + norm_floor),
        )
        smooth = smooth - scale_now * slope
    return smooth


def solution(mesh):
    return jax.shard_map(
        body,
        mesh=mesh,
        in_specs=(
            P("gz", "gx", None),
            P(None, "gz", None),
            P(),
            P(),
            P(None, "gz", "gx"),
            P(None, "gz", "gx"),
            P(None, "gz", "gx"),
            P(None, "gz", "gx"),
        ),
        out_specs=P("gz", "gx", None),
        check_vma=False,
    )
```

profile of v0, /device:TPU:1, one launch (start us, length us, event | category | flops | bytes accessed | tf_op | source)
XLA Modules:
  0.0 943.9 jit_solution(2549535672975663778)
XLA Ops:
  17.6 13.5 %while.60 = (s32[]{:T(128)}, f32[512,128]{1,0:T(8,128)S(1)}, f32[512,128]{1,0:T(8,128)}, s32[]{:T(128)}, s32[512]{0:T(512)S(1)}, /*index=5*/s32[512]{0:T(512)S(1...) while((s32[]{:T(128)}, f32[512,128]{1,0:T(8,128)S(1)}, ...), condition=%wide.region_4.5_spmd.clone, body=%wide.region_1.4_spmd.clone.sunk | while | flops 4265478 | bytes 13388487 | solution.py:94
  21.5 4.4 fusion.99
  36.0 180.4 %all-reduce.12.cloned.1.call-done = (bf16[512,128]{1,0:T(8,128)(2,1)}, bf16[512,128]{1,0:T(8,128)(2,1)}) async-done(((bf16[512,128]{1,0:T(8,128)(2,1)}, bf16[512,128]{1,0:T(8,128)(2,1)}), (bf16[512,128]{1,0:T(8,128)(2,1)}, bf16[512,128]{1,0:T(8,128)(2,1)})) %all-reduce.12.cloned.1.call-update) | async-done | bytes 262160 | tf_op jit(solution)/shard_map/psum | solution.py:100
  219.2 14.2 %while.61 = (s32[]{:T(128)}, f32[1024,128]{1,0:T(8,128)}, f32[1024,128]{1,0:T(8,128)}, s32[]{:T(128)}, s32[512]{0:T(512)S(1)}, /*index=5*/s32[512]{0:T(512)S(1)}...) while((s32[]{:T(128)}, f32[1024,128]{1,0:T(8,128)}, ...), condition=%wide.region_11.12_spmd.clone, body=%wide.region_8.11_spmd.clone.sunk | while | flops 4265478 | bytes 13912775 | solution.py:119
  223.0 3.4 fusion.104
  230.1 3.3 scatter_custom_fusion.47
  241.9 14.9 %while.62 = (s32[]{:T(128)}, f32[512,128]{1,0:T(8,128)}, f32[512,128]{1,0:T(8,128)}, s32[]{:T(128)}, s32[512]{0:T(512)S(1)}, /*index=5*/s32[512]{0:T(512)S(1)}, ...) while((s32[]{:T(128)}, f32[512,128]{1,0:T(8,128)}, ...), condition=%wide.region_15.16_spmd.clone, body=%wide.region_12.15_spmd.clone.sunk | while | flops 4265478 | bytes 13388487 | solution.py:94
  245.8 4.4 fusion.109
  260.8 227.1 %all-reduce.10.cloned.1.call-done = (bf16[512,128]{1,0:T(8,128)(2,1)}, bf16[512,128]{1,0:T(8,128)(2,1)}) async-done(((bf16[512,128]{1,0:T(8,128)(2,1)}, bf16[512,128]{1,0:T(8,128)(2,1)}), (bf16[512,128]{1,0:T(8,128)(2,1)}, bf16[512,128]{1,0:T(8,128)(2,1)})) %all-reduce.10.cloned.1.call-update) | async-done | bytes 262160 | tf_op jit(solution)/shard_map/psum | solution.py:100
  490.0 12.7 %while.63 = (s32[]{:T(128)}, f32[1024,128]{1,0:T(8,128)S(1)}, f32[1024,128]{1,0:T(8,128)}, s32[]{:T(128)}, s32[512]{0:T(512)S(1)}, /*index=5*/s32[512]{0:T(512)S...) while((s32[]{:T(128)}, f32[1024,128]{1,0:T(8,128)S(1)}, ...), condition=%wide.region_21.22_spmd.clone, body=%wide.region_18.21_spmd.clone.sunk | while | flops 4265478 | bytes 13912775 | solution.py:119
  493.8 3.4 fusion.114
  499.4 3.3 scatter_custom_fusion.55
  504.8 8.1 collective-permute-start
  521.3 3.4 collective-permute-done.3
  527.9 114.8 %all-reduce.4 = (f32[]{:T(128)}, f32[]{:T(128)}) all-reduce(f32[]{:T(128)} %get-tuple-element.839, f32[]{:T(128)} %get-tuple-element.837), channel_id=1, replica_groups=mesh['gz'=8,'gx'=32] {'gz','gx'}, use_global_device_ids=true, to_apply=%region_23.24 | all-reduce | flops 2 | bytes 16 | tf_op jit(solution)/shard_map/psum | solution.py:125
  644.2 3.3 collective-permute-start.4
  655.4 3.6 collective-permute-done.7
  662.3 77.8 %psum.69 = f32[]{:T(128)} all-reduce(f32[]{:T(128)} %get-tuple-element.833), channel_id=1, replica_groups=mesh['gz'=8,'gx'=32] {'gz','gx'}, use_global_device_ids=true, to_apply=%region_27.28 | all-reduce | flops 1 | bytes 8 | tf_op jit(solution)/shard_map/psum | solution.py:134
  740.8 3.3 collective-permute-start.8
  752.2 3.4 collective-permute-done.11
  758.8 79.0 %psum.70 = f32[]{:T(128)} all-reduce(f32[]{:T(128)} %get-tuple-element.829), channel_id=1, replica_groups=mesh['gz'=8,'gx'=32] {'gz','gx'}, use_global_device_ids=true, to_apply=%region_29.30 | all-reduce | flops 1 | bytes 8 | tf_op jit(solution)/shard_map/psum | solution.py:134
  838.6 3.4 collective-permute-start.12
  849.8 3.6 collective-permute-done.15
  856.6 78.8 %psum.71 = f32[]{:T(128)} all-reduce(f32[]{:T(128)} %get-tuple-element.825), channel_id=1, replica_groups=mesh['gz'=8,'gx'=32] {'gz','gx'}, use_global_device_ids=true, to_apply=%region_31.32 | all-reduce | flops 1 | bytes 8 | tf_op jit(solution)/shard_map/psum | solution.py:134
  (127 shorter events, 109.5 us)
Async XLA Ops:
  6.5 10.1 %copy-start.1 = (f32[32,16,256]{2,1,0:T(8,128)S(1)}, f32[32,16,256]{2,1,0:T(8,128)}, u32[]{:S(2)}) copy-start(f32[32,16,256]{2,1,0:T(8,128)} %param.16) | copy-start | bytes 1572868
  6.5 209.8 %all-reduce.12.cloned.1.call-start = ((), (), s32[]{:S(2)}) async-start(), calls=%async_computation.1 | async-start | bytes 524288 | tf_op jit(solution)/shard_map/psum | solution.py:100
  14.3 2.6 copy-start.3
  14.3 2.6 copy-start.4
  14.3 3.4 copy-start
  33.4 454.5 %all-reduce.10.cloned.1.call-start = ((), (), s32[]{:S(2)}) async-start(), calls=%async_computation | async-start | bytes 524288 | tf_op jit(solution)/shard_map/psum | solution.py:100
  502.6 1.3 copy-start.2
  504.8 10.0 %collective-permute-start = (f32[1,16,256]{2,1,0:T(8,128)S(1)}, f32[1,16,256]{2,1,0:T(8,128)S(1)}, u32[]{:S(2)}, u32[]{:S(2)}) collective-permute-start(f32[1,16,256]{2,1,0:T(8,128)S(1)} %get-tuple-element.879), channel_id=1, source_target_pairs={{0,32},{32,64},{64,96},{96,128},{128,160},{160,192},{192,224},{1,3... | collective-permute-start | bytes 49160 | tf_op jit(solution)/shard_map/ppermute | solution.py:23
  512.9 5.1 collective-permute-start.1
  518.0 3.3 collective-permute-start.2
  520.0 4.7 collective-permute-start.3
  644.2 5.3 collective-permute-start.4
  647.6 5.1 collective-permute-start.5
  652.7 2.7 collective-permute-start.6
  654.1 4.9 collective-permute-start.7
  740.8 5.3 collective-permute-start.8
  744.2 5.1 collective-permute-start.9
  749.3 2.9 collective-permute-start.10
  750.7 4.9 collective-permute-start.11
  838.6 5.3 collective-permute-start.12
  842.0 5.1 collective-permute-start.13
  847.1 2.8 collective-permute-start.14
  848.5 4.9 collective-permute-start.15
Sparse Core Ops, SparseCore 0:
  33.6 182.7 all-reduce.11
  260.2 227.7 all-reduce.9
where the time goes:
time: 947 us; the launch traced here: 944 us
  waiting for transfers between devices  434 us (46%)
  blocking collectives  350 us (37%)
  other arithmetic  55.2 us (6%)
  starting transfers between devices  37.5 us (4%)
  local copies, waits for them, and re-layouts  28.9 us (3%)
  between operations  22.3 us (2%)
  matrix products  15.6 us (2%)
    psum x2, waiting for transfers between devices, body(): lax.psum(ray_sum.astype(jnp.bfloat16), 'gx').astype(jnp.float32)  408 us
    psum x3, blocking collectives, body(): slope_total = lax.psum(slope_part, ('gz', 'gx'))  236 us
    psum x1, blocking collectives, body(): change_total = lax.psum(change_part, ('gz', 'gx'))  115 us
    ppermute x8, waiting for transfers between devices, padded_2(): lax.ppermute(head, axis, [((i + 1) % count, i) for i in range(ends)])  26.4 us
    ppermute x8, starting transfers between devices, padded_2(): lax.ppermute(tail, axis, [(i, (i + 1) % count) for i in range(ends)])  24.3 us
  transfers between devices with their start and end apart: 18, of which 10 were waited for; matrix products, arithmetic and copies ran while one was open for 0% of the time, Pallas kernels for 0%

commit v1 on v0

--- a/solution.py
+++ b/solution.py
@@ -1,6 +1,10 @@
+import functools
+
 import jax
 import jax.numpy as jnp
 from jax import lax
+from jax.experimental import pallas as pl
+from jax.experimental.pallas import tpu as pltpu
 from jax.sharding import PartitionSpec as P
 
 TV_STEPS = 4
@@ -10,6 +14,137 @@
 step_gain = 0.25
 norm_floor = 1e-06
 group_rows = 128
+
+
+MESH = pl.DeviceIdType.MESH
+
+
+def _peer(axis, position):
+    if axis == "gz":
+        return (position, lax.axis_index("gx"))
+    return (lax.axis_index("gz"), position)
+
+
+def vector_sum_kernel(n, x_ref, o_ref, recv, red, gath, ssem1, rsem1, ssem2, rsem2):
+    me = lax.axis_index("gx")
+    barrier = pltpu.get_barrier_semaphore()
+    for d in range(1, n):
+        pl.semaphore_signal(barrier, inc=1, device_id=_peer("gx", lax.rem(me + d, n)), device_id_type=MESH)
+    pl.semaphore_wait(barrier, n - 1)
+    sends = []
+    for d in range(1, n):
+        dst = lax.rem(me + d, n)
+        copy = pltpu.make_async_remote_copy(
+            src_ref=x_ref.at[dst], dst_ref=recv.at[d], send_sem=ssem1.at[d], recv_sem=rsem1.at[d],
+            device_id=_peer("gx", dst), device_id_type=MESH)
+        copy.start()
+        sends.append(copy)
+    for copy in sends:
+        copy.wait()
+    total = x_ref[me].astype(jnp.float32)
+    for d in range(1, n):
+        total = total + recv[d].astype(jnp.float32)
+    red[...] = total.astype(red.dtype)
+    sends = []
+    for d in range(1, n):
+        dst = lax.rem(me + d, n)
+        copy = pltpu.make_async_remote_copy(
+            src_ref=red, dst_ref=gath.at[me], send_sem=ssem2.at[d], recv_sem=rsem2.at[d],
+            device_id=_peer("gx", dst), device_id_type=MESH)
+        copy.start()
+        sends.append(copy)
+    for copy in sends:
+        copy.wait()
+    gath[me] = red[...]
+    o_ref[...] = gath[...]
+
+
+def vector_sum(x):
+    n, rows, cols = x.shape
+    return pl.pallas_call(
+        functools.partial(vector_sum_kernel, n),
+        out_shape=jax.ShapeDtypeStruct(x.shape, x.dtype),
+        in_specs=[pl.BlockSpec(memory_space=pltpu.VMEM)],
+        out_specs=pl.BlockSpec(memory_space=pltpu.VMEM),
+        scratch_shapes=[
+            pltpu.VMEM(x.shape, x.dtype),
+            pltpu.VMEM((rows, cols), x.dtype),
+            pltpu.VMEM(x.shape, x.dtype),
+            pltpu.SemaphoreType.DMA((n,)),
+            pltpu.SemaphoreType.DMA((n,)),
+            pltpu.SemaphoreType.DMA((n,)),
+            pltpu.SemaphoreType.DMA((n,)),
+        ],
+        compiler_params=pltpu.CompilerParams(collective_id=1, has_side_effects=True),
+    )(x)
+
+
+def _stage_peers(stage):
+    axis, stride, size = stage
+    index = lax.axis_index(axis)
+    position = lax.rem(index // stride, size)
+    base = index - position * stride
+    return [base + lax.rem(position + d, size) * stride for d in range(1, size)]
+
+
+def scalar_sum_kernel(stages, x_ref, o_ref, buf, recv, ssem, rsem):
+    barrier = pltpu.get_barrier_semaphore()
+    count = 0
+    for stage in stages:
+        for peer in _stage_peers(stage):
+            pl.semaphore_signal(barrier, inc=1, device_id=_peer(stage[0], peer), device_id_type=MESH)
+            count += 1
+    pl.semaphore_wait(barrier, count)
+    total = x_ref[...]
+    slot = 0
+    for s, stage in enumerate(stages):
+        source = x_ref if s == 0 else buf.at[s - 1]
+        sends = []
+        for d, peer in enumerate(_stage_peers(stage)):
+            copy = pltpu.make_async_remote_copy(
+                src_ref=source, dst_ref=recv.at[slot + d], send_sem=ssem.at[slot + d],
+                recv_sem=rsem.at[slot + d], device_id=_peer(stage[0], peer), device_id_type=MESH)
+            copy.start()
+            sends.append(copy)
+        for copy in sends:
+            copy.wait()
+        for d in range(len(sends)):
+            total = total + recv[slot + d]
+        slot += len(sends)
+        if s + 1 < len(stages):
+            buf[s] = total
+    o_ref[...] = total
+
+
+def scalar_sum(x, stages):
+    slots = sum(size - 1 for _, _, size in stages)
+    return pl.pallas_call(
+        functools.partial(scalar_sum_kernel, stages),
+        out_shape=jax.ShapeDtypeStruct(x.shape, x.dtype),
+        in_specs=[pl.BlockSpec(memory_space=pltpu.VMEM)],
+        out_specs=pl.BlockSpec(memory_space=pltpu.VMEM),
+        scratch_shapes=[
+            pltpu.VMEM((max(len(stages) - 1, 1),) + x.shape, x.dtype),
+            pltpu.VMEM((slots,) + x.shape, x.dtype),
+            pltpu.SemaphoreType.DMA((slots,)),
+            pltpu.SemaphoreType.DMA((slots,)),
+        ],
+        compiler_params=pltpu.CompilerParams(collective_id=2, has_side_effects=True),
+    )(x)
+
+
+def scalar_stages(n_gz, n_gx):
+    stages = [("gz", 1, n_gz)]
+    if n_gx % 4 == 0 and n_gx > 4:
+        stages += [("gx", 1, 4), ("gx", 4, n_gx // 4)]
+    else:
+        stages += [("gx", 1, n_gx)]
+    return [stage for stage in stages if stage[2] > 1]
+
+
+def pack_pair(a, b):
+    lane = lax.broadcasted_iota(jnp.int32, (8, 128), 1)
+    return jnp.where(lane == 0, a, jnp.where(lane == 1, b, 0.0)).astype(jnp.float32)
 
 
 def padded_2(cells, sides, width):
@@ -95,10 +230,11 @@
         target = lax.dynamic_index_in_dim(measured, view_index, 0, keepdims=False).reshape(
             slab_tiles, group_rows
         )
-        projection, ray_sum = (
-            lax.psum(projection.astype(jnp.bfloat16), "gx").astype(jnp.float32),
-            lax.psum(ray_sum.astype(jnp.bfloat16), "gx").astype(jnp.float32),
-        )
+        n_gx = lax.axis_size("gx")
+        joined = jnp.concatenate([projection, ray_sum], axis=1).astype(jnp.bfloat16)
+        joined = vector_sum(joined.reshape(n_gx, slab_tiles // n_gx, 2 * group_rows))
+        joined = joined.reshape(slab_tiles, 2 * group_rows).astype(jnp.float32)
+        projection, ray_sum = joined[:, :group_rows], joined[:, group_rows:]
         residual = ((target - projection) / (ray_sum + 1.0)).astype(jnp.bfloat16)
 
         def backward(index, carry):
@@ -121,21 +257,20 @@
     art_volume = jnp.maximum(current, 0.0)
     difference = art_volume - volume
     change_part = jnp.sum(difference * difference)
+    stages = scalar_stages(lax.axis_size("gz"), lax.axis_size("gx"))
+    smooth = art_volume
     change_total = None
-    change_total = lax.psum(change_part, ("gz", "gx"))
-    smooth = art_volume
     for sweep_index in range(TV_STEPS):
         padded = padded_2(smooth, (("gz", 0), ("gx", 1)), 1)
         slope = tv_grad(pad_depth(padded))
         slope_part = jnp.sum(slope * slope)
         if sweep_index == 0:
-            slope_total = lax.psum(slope_part, ("gz", "gx"))
+            totals = scalar_sum(pack_pair(slope_part, change_part), stages)
+            change_total = totals[0, 1]
         else:
-            slope_total = lax.psum(slope_part, ("gz", "gx"))
-        change_total, scale_now = (
-            change_total,
-            step_gain * jnp.sqrt(change_total) / jnp.sqrt(slope_total + norm_floor),
-        )
+            totals = scalar_sum(pack_pair(slope_part, 0.0), stages)
+        slope_total = totals[0, 0]
+        scale_now = step_gain * jnp.sqrt(change_total) / jnp.sqrt(slope_total + norm_floor)
         smooth = smooth - scale_now * slope
     return smooth
 

time: 947 us -> 471 us (0.50)
  waiting for transfers between devices: 434 us -> 25.1 us
  blocking collectives: 350 us -> 0 us
  Pallas kernels: 0 us -> 284 us
  between operations: 22.3 us -> 9.15 us
    psum x2 -> x0, waiting for transfers between devices: 408 us -> none  [body(): lax.psum(ray_sum.astype(jnp.bfloat16), 'gx').astype(jnp.float32)]
    psum x4 -> x0, blocking collectives: 350 us -> none  [the longest x3 236 us: body(): slope_total = lax.psum(slope_part, ('gz', 'gx'))]
    pallas_call x0 -> x6, Pallas kernels: none -> 284 us  [the longest x2 171 us: vector_sum(): pl.pallas_call(functools.partial(vector_sum_kernel, n), out_shape=jax.Sha...]
  transfers between devices with their start and end apart: 18 -> 16, of which waited for: 10 -> 8; matrix products, arithmetic and copies ran while one was open for 0% -> 0% of each run, Pallas kernels for 0% -> 0%
where the time goes in v1:
time: 471 us; the launch traced here: 468 us
  Pallas kernels  284 us (60%)
  other arithmetic  58.1 us (12%)
  starting transfers between devices  41.9 us (9%)
  local copies, waits for them, and re-layouts  34.1 us (7%)
  waiting for transfers between devices  25.1 us (5%)
  matrix products  15.6 us (3%)
  between operations  9.15 us (2%)
    pallas_call x2, Pallas kernels, vector_sum(): pl.pallas_call(functools.partial(vector_sum_kernel, n), out_shape=jax.Sha...  171 us
    pallas_call x4, Pallas kernels, scalar_sum(): pl.pallas_call(functools.partial(scalar_sum_kernel, stages), out_shape=ja...  113 us
    ppermute x8, starting transfers between devices, padded_2(): lax.ppermute(tail, axis, [(i, (i + 1) % count) for i in range(ends)])  28.8 us
    ppermute x8, waiting for transfers between devices, padded_2(): lax.ppermute(head, axis, [((i + 1) % count, i) for i in range(ends)])  25.1 us
    ppermute x8, starting transfers between devices, padded_2(): lax.ppermute(head, axis, [((i + 1) % count, i) for i in range(ends)])  13.1 us
  transfers between devices with their start and end apart: 16, of which 8 were waited for; matrix products, arithmetic and copies ran while one was open for 0% of the time, Pallas kernels for 0%

profile of v1, /device:TPU:1, one launch (start us, length us, event | category | flops | bytes accessed | tf_op | source)
XLA Modules:
  0.0 468.4 jit_solution(12318104602314870312)
XLA Ops:
  11.9 13.5 %while.60 = (s32[]{:T(128)}, f32[512,128]{1,0:T(8,128)S(1)}, f32[512,128]{1,0:T(8,128)}, s32[]{:T(128)}, s32[512]{0:T(512)S(1)}, /*index=5*/s32[512]{0:T(512)S(1...) while((s32[]{:T(128)}, f32[512,128]{1,0:T(8,128)S(1)}, ...), condition=%wide.region_4.5_spmd.clone, body=%wide.region_1.4_spmd.clone.sunk | while | flops 4265478 | bytes 13388487 | solution.py:229
  15.7 4.4 fusion.104
  27.1 67.9 %shard_map.82 = bf16[32,16,256]{2,1,0:T(8,128)(2,1)} custom-call(bf16[32,16,256]{2,1,0:T(8,128)(2,1)} %pad_maximum_fusion.x_ref), custom_call_target="tpu_custom_call" | custom-call | tf_op jit(solution)/shard_map/pallas_call | solution.py:64
  101.4 14.2 %while.61 = (s32[]{:T(128)}, f32[1024,128]{1,0:T(8,128)}, f32[1024,128]{1,0:T(8,128)}, s32[]{:T(128)}, s32[512]{0:T(512)S(1)}, /*index=5*/s32[512]{0:T(512)S(1)}...) while((s32[]{:T(128)}, f32[1024,128]{1,0:T(8,128)}, ...), condition=%wide.region_9.10_spmd.clone, body=%wide.region_6.9_spmd.clone.sunk | while | flops 4265478 | bytes 13912775 | solution.py:255
  105.2 3.4 fusion.109
  112.3 3.3 scatter_custom_fusion.47
  122.4 13.5 %while.62 = (s32[]{:T(128)}, f32[512,128]{1,0:T(8,128)S(1)}, f32[512,128]{1,0:T(8,128)}, s32[]{:T(128)}, s32[512]{0:T(512)S(1)}, /*index=5*/s32[512]{0:T(512)S(1...) while((s32[]{:T(128)}, f32[512,128]{1,0:T(8,128)S(1)}, ...), condition=%wide.region_13.14_spmd.clone, body=%wide.region_10.13_spmd.clone.sunk | while | flops 4265478 | bytes 13388487 | solution.py:229
  126.3 4.4 fusion.114
  137.7 103.3 %shard_map.83 = bf16[32,16,256]{2,1,0:T(8,128)(2,1)} custom-call(bf16[32,16,256]{2,1,0:T(8,128)(2,1)} %pad_maximum_fusion.1.x_ref), custom_call_target="tpu_custom_call" | custom-call | tf_op jit(solution)/shard_map/pallas_call | solution.py:64
  244.6 12.7 %while.63 = (s32[]{:T(128)}, f32[1024,128]{1,0:T(8,128)S(1)}, f32[1024,128]{1,0:T(8,128)}, s32[]{:T(128)}, s32[512]{0:T(512)S(1)}, /*index=5*/s32[512]{0:T(512)S...) while((s32[]{:T(128)}, f32[1024,128]{1,0:T(8,128)S(1)}, ...), condition=%wide.region_17.18_spmd.clone, body=%wide.region_14.17_spmd.clone.sunk | while | flops 4265478 | bytes 13912775 | solution.py:255
  248.4 3.4 fusion.119
  254.0 3.3 scatter_custom_fusion.55
  259.4 6.8 %collective-permute-start = (f32[1,16,256]{2,1,0:T(8,128)S(1)}, f32[1,16,256]{2,1,0:T(8,128)S(1)}, u32[]{:S(2)}, u32[]{:S(2)}) collective-permute-start(f32[1,16,256]{2,1,0:T(8,128)S(1)} %get-tuple-element.873), channel_id=1, source_target_pairs={{0,32},{32,64},{64,96},{96,128},{128,160},{160,192},{192,224},{1,3... | collective-permute-start | bytes 49160 | tf_op jit(solution)/shard_map/ppermute | solution.py:158
  283.3 56.3 %shard_map.84 = f32[8,128]{1,0:T(8,128)} custom-call(f32[8,128]{1,0:T(8,128)} %broadcast_select_fusion.x_ref), custom_call_target="tpu_custom_call" | custom-call | tf_op jit(solution)/shard_map/pallas_call | solution.py:121
  347.4 3.1 collective-permute-done.5
  354.6 3.1 collective-permute-done.7
  362.2 19.2 %shard_map.85 = f32[8,128]{1,0:T(8,128)} custom-call(f32[8,128]{1,0:T(8,128)} %iota.45.x_ref), custom_call_target="tpu_custom_call" | custom-call | tf_op jit(solution)/shard_map/pallas_call | solution.py:121
  383.5 4.3 collective-permute-start.8
  396.7 3.4 collective-permute-done.11
  404.6 19.0 %shard_map.86 = f32[8,128]{1,0:T(8,128)} custom-call(f32[8,128]{1,0:T(8,128)} %iota.46.x_ref), custom_call_target="tpu_custom_call" | custom-call | tf_op jit(solution)/shard_map/pallas_call | solution.py:121
  425.6 4.5 collective-permute-start.12
  432.1 3.1 collective-permute-done.13
  439.0 3.4 collective-permute-done.15
  446.9 18.7 %shard_map.87 = f32[8,128]{1,0:T(8,128)} custom-call(f32[8,128]{1,0:T(8,128)} %iota.47.x_ref), custom_call_target="tpu_custom_call" | custom-call | tf_op jit(solution)/shard_map/pallas_call | solution.py:121
  (142 shorter events, 120.9 us)
Async XLA Ops:
  0.0 10.9 %copy-start.1 = (f32[32,16,256]{2,1,0:T(8,128)S(1)}, f32[32,16,256]{2,1,0:T(8,128)}, u32[]{:S(2)}) copy-start(f32[32,16,256]{2,1,0:T(8,128)} %param.16) | copy-start | bytes 1572868
  8.5 2.6 copy-start.4
  8.5 2.6 copy-start.5
  8.5 3.4 copy-start
  135.9 106.0 %copy-start.3 = (f32[1,32,2048]{2,1,0:T(8,128)S(1)}, f32[1,32,2048]{2,1,0:T(8,128)}, u32[]{:S(2)}) copy-start(f32[1,32,2048]{2,1,0:T(8,128)} %get-tuple-element.875) | copy-start | bytes 786436
  257.3 1.3 copy-start.2
  259.4 8.7 %collective-permute-start = (f32[1,16,256]{2,1,0:T(8,128)S(1)}, f32[1,16,256]{2,1,0:T(8,128)S(1)}, u32[]{:S(2)}, u32[]{:S(2)}) collective-permute-start(f32[1,16,256]{2,1,0:T(8,128)S(1)} %get-tuple-element.873), channel_id=1, source_target_pairs={{0,32},{32,64},{64,96},{96,128},{128,160},{160,192},{192,224},{1,3... | collective-permute-start | bytes 49160 | tf_op jit(solution)/shard_map/ppermute | solution.py:158
  266.2 5.1 %collective-permute-start.1 = (f32[1,16,256]{2,1,0:T(8,128)S(1)}, f32[1,16,256]{2,1,0:T(8,128)S(1)}, u32[]{:S(2)}, u32[]{:S(2)}) collective-permute-start(f32[1,16,256]{2,1,0:T(8,128)S(1)} %get-tuple-element.874), channel_id=1, source_target_pairs={{32,0},{64,32},{96,64},{128,96},{160,128},{192,160},{224,192},{33,... | collective-permute-start | bytes 49160 | tf_op jit(solution)/shard_map/ppermute | solution.py:160
  271.3 4.7 %collective-permute-start.2 = (f32[34,1,256]{2,1,0:T(1,128)S(1)}, f32[34,1,256]{2,1,0:T(1,128)S(1)}, u32[]{:S(2)}, u32[]{:S(2)}) collective-permute-start(f32[34,1,256]{2,1,0:T(1,128)S(1)} %get-tuple-element.865), channel_id=1, source_target_pairs={{0,1},{1,2},{2,3},{3,4},{4,5},{5,6},{6,7},{7,8},{8,9},{9,10},{10,1... | collective-permute-start | bytes 104456 | tf_op jit(solution)/shard_map/ppermute | solution.py:158
  274.1 4.7 collective-permute-start.3
  342.5 4.9 %collective-permute-start.4 = (f32[1,16,256]{2,1,0:T(8,128)S(1)}, f32[1,16,256]{2,1,0:T(8,128)S(1)}, u32[]{:S(2)}, u32[]{:S(2)}) collective-permute-start(f32[1,16,256]{2,1,0:T(8,128)S(1)} %get-tuple-element.871), channel_id=1, source_target_pairs={{0,32},{32,64},{64,96},{96,128},{128,160},{160,192},{192,224},{1,3... | collective-permute-start | bytes 49160 | tf_op jit(solution)/shard_map/ppermute | solution.py:158
  345.4 5.1 %collective-permute-start.5 = (f32[1,16,256]{2,1,0:T(8,128)S(1)}, f32[1,16,256]{2,1,0:T(8,128)S(1)}, u32[]{:S(2)}, u32[]{:S(2)}) collective-permute-start(f32[1,16,256]{2,1,0:T(8,128)S(1)} %get-tuple-element.872), channel_id=1, source_target_pairs={{32,0},{64,32},{96,64},{128,96},{160,128},{192,160},{224,192},{33,... | collective-permute-start | bytes 49160 | tf_op jit(solution)/shard_map/ppermute | solution.py:160
  350.6 4.0 collective-permute-start.6
  353.0 4.7 collective-permute-start.7
  383.5 6.3 %collective-permute-start.8 = (f32[1,16,256]{2,1,0:T(8,128)S(1)}, f32[1,16,256]{2,1,0:T(8,128)S(1)}, u32[]{:S(2)}, u32[]{:S(2)}) collective-permute-start(f32[1,16,256]{2,1,0:T(8,128)S(1)} %get-tuple-element.869), channel_id=1, source_target_pairs={{0,32},{32,64},{64,96},{96,128},{128,160},{160,192},{192,224},{1,3... | collective-permute-start | bytes 49160 | tf_op jit(solution)/shard_map/ppermute | solution.py:158
  387.8 5.1 %collective-permute-start.9 = (f32[1,16,256]{2,1,0:T(8,128)S(1)}, f32[1,16,256]{2,1,0:T(8,128)S(1)}, u32[]{:S(2)}, u32[]{:S(2)}) collective-permute-start(f32[1,16,256]{2,1,0:T(8,128)S(1)} %get-tuple-element.870), channel_id=1, source_target_pairs={{32,0},{64,32},{96,64},{128,96},{160,128},{192,160},{224,192},{33,... | collective-permute-start | bytes 49160 | tf_op jit(solution)/shard_map/ppermute | solution.py:160
  392.9 3.8 collective-permute-start.10
  395.4 4.7 collective-permute-start.11
  425.6 6.4 %collective-permute-start.12 = (f32[1,16,256]{2,1,0:T(8,128)S(1)}, f32[1,16,256]{2,1,0:T(8,128)S(1)}, u32[]{:S(2)}, u32[]{:S(2)}) collective-permute-start(f32[1,16,256]{2,1,0:T(8,128)S(1)} %get-tuple-element.867), channel_id=1, source_target_pairs={{0,32},{32,64},{64,96},{96,128},{128,160},{160,192},{192,224},{1,3... | collective-permute-start | bytes 49160 | tf_op jit(solution)/shard_map/ppermute | solution.py:158
  430.1 5.1 %collective-permute-start.13 = (f32[1,16,256]{2,1,0:T(8,128)S(1)}, f32[1,16,256]{2,1,0:T(8,128)S(1)}, u32[]{:S(2)}, u32[]{:S(2)}) collective-permute-start(f32[1,16,256]{2,1,0:T(8,128)S(1)} %get-tuple-element.868), channel_id=1, source_target_pairs={{32,0},{64,32},{96,64},{128,96},{160,128},{192,160},{224,192},{33,... | collective-permute-start | bytes 49160 | tf_op jit(solution)/shard_map/ppermute | solution.py:160
  435.2 3.8 collective-permute-start.14
  437.7 4.7 collective-permute-start.15

commit v2 on v1

--- a/solution.py
+++ b/solution.py
@@ -147,6 +147,41 @@
     return jnp.where(lane == 0, a, jnp.where(lane == 1, b, 0.0)).astype(jnp.float32)
 
 
+def one_hot(index, size):
+    return (index[:, None] == jnp.arange(size, dtype=jnp.int32)[None, :]).astype(jnp.bfloat16)
+
+
+def block_apply_kernel(transposed, x_ref, blk_ref, w_ref, o_ref):
+    o_ref[...] = jnp.zeros_like(o_ref)
+    x = x_ref[...]
+    chosen = blk_ref[...]
+
+    def step(b, carry):
+        masked = jnp.where(chosen == b, x, jnp.zeros_like(x))
+        if transposed:
+            dims = (((1,), (1,)), ((), ()))
+        else:
+            dims = (((1,), (0,)), ((), ()))
+        o_ref[...] += lax.dot_general(masked, w_ref[b], dims, preferred_element_type=jnp.float32)
+        return carry
+
+    lax.fori_loop(0, w_ref.shape[0], step, 0)
+
+
+def block_apply(x, chosen, weights, transposed):
+    entries, width = x.shape
+    n_blocks = weights.shape[0]
+    return pl.pallas_call(
+        functools.partial(block_apply_kernel, transposed),
+        out_shape=jax.ShapeDtypeStruct((entries, width), jnp.float32),
+        in_specs=[pl.BlockSpec(memory_space=pltpu.VMEM)] * 3,
+        out_specs=pl.BlockSpec(memory_space=pltpu.VMEM),
+        cost_estimate=pl.CostEstimate(
+            flops=2 * entries * width * width * n_blocks, transcendentals=0,
+            bytes_accessed=weights.size * 2 + entries * width * 10),
+    )(x, chosen, weights)
+
+
 def padded_2(cells, sides, width):
     for axis, dim in sides:
         count = lax.axis_size(axis)
@@ -191,7 +226,7 @@
     plane_tiles = depth_x * tiles_y
     row_weight = jnp.sum(weight_blocks, axis=2, dtype=jnp.float32)
     col_weight = jnp.sum(weight_blocks, axis=1, dtype=jnp.float32)
-    offsets = jnp.arange(group_rows, dtype=jnp.int32)
+    n_blocks = weight_blocks.shape[0]
     current = volume
     for turn_index in range(view_order.shape[0]):
         view_index = view_order[turn_index]
@@ -199,34 +234,24 @@
         column_list = lax.dynamic_index_in_dim(tile_column, view_index, 0, keepdims=False)[0]
         block_list = lax.dynamic_index_in_dim(tile_block, view_index, 0, keepdims=False)[0]
         live_count = lax.dynamic_index_in_dim(entry_count, view_index, 0, keepdims=False)[0, 0]
-        rounds = (live_count + group_rows - 1) // group_rows
+        entries = voxel_list.shape[0]
+        live = (jnp.arange(entries, dtype=jnp.int32) < live_count)[:, None]
+        detector = voxel_list // plane_tiles * tiles_u + column_list
         voxel_tiles = current.astype(jnp.bfloat16).reshape(-1, group_rows)
-
-        def gather_group(index):
-            begin = index * group_rows
-            voxels = lax.dynamic_slice_in_dim(voxel_list, begin, group_rows)
-            columns = lax.dynamic_slice_in_dim(column_list, begin, group_rows)
-            chosen = lax.dynamic_slice_in_dim(block_list, begin, group_rows)
-            weight = (begin + offsets < live_count).astype(jnp.float32)[:, None]
-            detector = voxels // plane_tiles * tiles_u + columns
-            return (voxels, detector, chosen, weight)
-
-        def forward(index, carry):
-            projection, ray_sum = carry
-            voxels, detector, chosen, weight = gather_group(index)
-            product = jnp.einsum(
-                "ejk,ek->ej",
-                weight_blocks[chosen],
-                voxel_tiles[voxels],
-                preferred_element_type=jnp.float32,
-            )
-            return (
-                projection.at[detector].add(product * weight),
-                ray_sum.at[detector].add(row_weight[chosen] * weight),
-            )
-
-        empty = jnp.zeros((slab_tiles, group_rows), jnp.float32)
-        projection, ray_sum = lax.fori_loop(0, rounds, forward, (empty, empty))
+        pick_voxel = one_hot(voxel_list, voxel_tiles.shape[0])
+        pick_detector = one_hot(detector, slab_tiles)
+        pick_block = jnp.where(live, one_hot(block_list, n_blocks), 0)
+        blocks_column = block_list[:, None]
+
+        cells = jnp.dot(pick_voxel, voxel_tiles, preferred_element_type=jnp.float32)
+        product = block_apply(cells.astype(jnp.bfloat16), blocks_column, weight_blocks, True)
+        product = jnp.where(live, product, 0.0)
+        projection = lax.dot_general(
+            pick_detector.astype(jnp.float32), product, (((0,), (0,)), ((), ())),
+            precision=lax.Precision.HIGHEST)
+        detector_blocks = lax.dot_general(
+            pick_detector, pick_block, (((0,), (0,)), ((), ())), preferred_element_type=jnp.float32)
+        ray_sum = jnp.dot(detector_blocks, row_weight, precision=lax.Precision.HIGHEST)
         target = lax.dynamic_index_in_dim(measured, view_index, 0, keepdims=False).reshape(
             slab_tiles, group_rows
         )
@@ -237,22 +262,15 @@
         projection, ray_sum = joined[:, :group_rows], joined[:, group_rows:]
         residual = ((target - projection) / (ray_sum + 1.0)).astype(jnp.bfloat16)
 
-        def backward(index, carry):
-            change, voxel_sum = carry
-            voxels, detector, chosen, weight = gather_group(index)
-            product = jnp.einsum(
-                "ejk,ej->ek",
-                weight_blocks[chosen],
-                residual[detector],
-                preferred_element_type=jnp.float32,
-            )
-            return (
-                change.at[voxels].add(product * weight),
-                voxel_sum.at[voxels].add(col_weight[chosen] * weight),
-            )
-
-        blank = jnp.zeros((voxel_tiles.shape[0], group_rows), jnp.float32)
-        change, voxel_sum = lax.fori_loop(0, rounds, backward, (blank, blank))
+        pixels = jnp.dot(pick_detector, residual, preferred_element_type=jnp.float32)
+        product = block_apply(pixels.astype(jnp.bfloat16), blocks_column, weight_blocks, False)
+        product = jnp.where(live, product, 0.0)
+        change = lax.dot_general(
+            pick_voxel.astype(jnp.float32), product, (((0,), (0,)), ((), ())),
+            precision=lax.Precision.HIGHEST)
+        voxel_blocks = lax.dot_general(
+            pick_voxel, pick_block, (((0,), (0,)), ((), ())), preferred_element_type=jnp.float32)
+        voxel_sum = jnp.dot(voxel_blocks, col_weight, precision=lax.Precision.HIGHEST)
         current = current + (change / (voxel_sum + 1.0)).reshape(current.shape)
     art_volume = jnp.maximum(current, 0.0)
     difference = art_volume - volume

time: 471 us -> 339 us (0.72)
  Pallas kernels: 284 us -> 205 us
  other arithmetic: 58.1 us -> 25.7 us
  local copies, waits for them, and re-layouts: 34.1 us -> 12.5 us
    pallas_call x2, Pallas kernels: 171 us -> 51.7 us  [vector_sum(): pl.pallas_call(functools.partial(vector_sum_kernel, n), out_shape=jax.Sha...]
    pallas_call x0 -> x4, Pallas kernels: none -> 77.2 us  [block_apply(): pl.pallas_call(functools.partial(block_apply_kernel, transposed), out_sha...]
    pallas_call x4, Pallas kernels: 113 us -> 76.1 us  [scalar_sum(): pl.pallas_call(functools.partial(scalar_sum_kernel, stages), out_shape=ja...]
    scatter-add x8 -> x0, other arithmetic: 20.2 us -> none  [the longest x2 6.53 us: backward(): voxel_sum.at[voxels].add(col_weight[chosen] * weight)]
    gather x8 -> x0, local copies, waits for them, and re-layouts: 15 us -> none  [the longest x2 6.06 us: forward(): weight_blocks[chosen]]
    convert_element_type x6 -> x0, other arithmetic: 4.71 us -> none  [the longest x4 2.63 us: gather_group(): weight = (begin + offsets < live_count).astype(jnp.float32)[:, None]]
    dot_general x4 -> x16, matrix products: 15.6 us -> 19.5 us  [the longest x2 5.89 us: body(): lax.dot_general(pick_voxel.astype(jnp.float32), product, (((0,), (0,)), (...]
where the time goes in v2:
time: 339 us; the launch traced here: 338 us
  Pallas kernels  205 us (60%)
  starting transfers between devices  42.1 us (12%)
  other arithmetic  25.7 us (8%)
  waiting for transfers between devices  25 us (7%)
  matrix products  19.5 us (6%)
  local copies, waits for them, and re-layouts  12.5 us (4%)
  between operations  8.05 us (2%)
    pallas_call x4, Pallas kernels, block_apply(): pl.pallas_call(functools.partial(block_apply_kernel, transposed), out_sha...  77.2 us
    pallas_call x4, Pallas kernels, scalar_sum(): pl.pallas_call(functools.partial(scalar_sum_kernel, stages), out_shape=ja...  76.1 us
    pallas_call x2, Pallas kernels, vector_sum(): pl.pallas_call(functools.partial(vector_sum_kernel, n), out_shape=jax.Sha...  51.7 us
    ppermute x8, starting transfers between devices, padded_2(): lax.ppermute(tail, axis, [(i, (i + 1) % count) for i in range(ends)])  28.9 us
    ppermute x8, waiting for transfers between devices, padded_2(): lax.ppermute(head, axis, [((i + 1) % count, i) for i in range(ends)])  25 us
    ppermute x8, starting transfers between devices, padded_2(): lax.ppermute(head, axis, [((i + 1) % count, i) for i in range(ends)])  13.1 us
  transfers between devices with their start and end apart: 16, of which 8 were waited for; matrix products, arithmetic and copies ran while one was open for 0% of the time, Pallas kernels for 0%

profile of v2, /device:TPU:1, one launch (start us, length us, event | category | flops | bytes accessed | tf_op | source)
XLA Modules:
  0.0 337.8 jit_solution(11016148093079998063)
XLA Ops:
  13.7 19.3 %shard_map.82 = f32[512,128]{1,0:T(8,128)} custom-call(bf16[512,128]{1,0:T(8,128)(2,1)} %fusion.9.x_ref, s32[512,1]{1,0:T(8,128)} %copy.11.blk_ref, bf16[64,128,128]{2,1,0:T(8,128)(2,1)} %w_ref.7), custom_call_target="tpu_custom_call" | custom-call | flops 1073741824 | bytes 2752512 | tf_op jit(solution)/shard_map/pallas_call | solution.py:174
  36.2 28.7 %shard_map.83 = bf16[32,16,256]{2,1,0:T(8,128)(2,1)} custom-call(bf16[32,16,256]{2,1,0:T(8,128)(2,1)} %pad_maximum_fusion.x_ref), custom_call_target="tpu_custom_call" | custom-call | tf_op jit(solution)/shard_map/pallas_call | solution.py:64
  67.1 19.2 %shard_map.84 = f32[512,128]{1,0:T(8,128)} custom-call(bf16[512,128]{1,0:T(8,128)(2,1)} %convolution_convert_fusion.2.x_ref, s32[512,1]{1,0:T(8,128)} %copy.11.blk_ref, bf16[64,128,128]{2,1,0:T(8,128)(2,1)} %w_ref.7), custom_call_target="tpu_custom_call" | custom-call | flops 1073741824 | bytes 2752512 | tf_op jit(solution)/shard_map/pallas_call | solution.py:174
  86.9 3.0 fusion.7
  94.6 19.2 %shard_map.85 = f32[512,128]{1,0:T(8,128)} custom-call(bf16[512,128]{1,0:T(8,128)(2,1)} %fusion.10.x_ref, s32[512,1]{1,0:T(8,128)} %copy.14.blk_ref, bf16[64,128,128]{2,1,0:T(8,128)(2,1)} %w_ref.7), custom_call_target="tpu_custom_call" | custom-call | flops 1073741824 | bytes 2752512 | tf_op jit(solution)/shard_map/pallas_call | solution.py:174
  117.0 23.0 %shard_map.86 = bf16[32,16,256]{2,1,0:T(8,128)(2,1)} custom-call(bf16[32,16,256]{2,1,0:T(8,128)(2,1)} %pad_maximum_fusion.1.x_ref), custom_call_target="tpu_custom_call" | custom-call | tf_op jit(solution)/shard_map/pallas_call | solution.py:64
  142.0 19.4 %shard_map.87 = f32[512,128]{1,0:T(8,128)} custom-call(bf16[512,128]{1,0:T(8,128)(2,1)} %convolution_convert_fusion.x_ref, s32[512,1]{1,0:T(8,128)} %copy.14.blk_ref, bf16[64,128,128]{2,1,0:T(8,128)(2,1)} %w_ref.7), custom_call_target="tpu_custom_call" | custom-call | flops 1073741824 | bytes 2752512 | tf_op jit(solution)/shard_map/pallas_call | solution.py:174
  162.0 2.9 fusion.8
  165.9 6.1 %collective-permute-start = (f32[1,16,256]{2,1,0:T(8,128)S(1)}, f32[1,16,256]{2,1,0:T(8,128)S(1)}, u32[]{:S(2)}, u32[]{:S(2)}) collective-permute-start(f32[1,16,256]{2,1,0:T(8,128)S(1)} %get-tuple-element.49), channel_id=1, source_target_pairs={{0,32},{32,64},{64,96},{96,128},{128,160},{160,192},{192,224},{1,3... | collective-permute-start | bytes 49160 | tf_op jit(solution)/shard_map/ppermute | solution.py:193
  174.0 3.1 collective-permute-done.1
  181.7 2.7 collective-permute-done.3
  189.0 20.1 %shard_map.88 = f32[8,128]{1,0:T(8,128)} custom-call(f32[8,128]{1,0:T(8,128)} %broadcast_select_fusion.x_ref), custom_call_target="tpu_custom_call" | custom-call | tf_op jit(solution)/shard_map/pallas_call | solution.py:121
  211.9 4.0 %collective-permute-start.4 = (f32[1,16,256]{2,1,0:T(8,128)S(1)}, f32[1,16,256]{2,1,0:T(8,128)S(1)}, u32[]{:S(2)}, u32[]{:S(2)}) collective-permute-start(f32[1,16,256]{2,1,0:T(8,128)S(1)} %get-tuple-element.47), channel_id=1, source_target_pairs={{0,32},{32,64},{64,96},{96,128},{128,160},{160,192},{192,224},{1,3... | collective-permute-start | bytes 49160 | tf_op jit(solution)/shard_map/ppermute | solution.py:193
  217.8 3.1 collective-permute-done.5
  224.8 3.4 collective-permute-done.7
  232.6 18.3 %shard_map.89 = f32[8,128]{1,0:T(8,128)} custom-call(f32[8,128]{1,0:T(8,128)} %iota.59.x_ref), custom_call_target="tpu_custom_call" | custom-call | tf_op jit(solution)/shard_map/pallas_call | solution.py:121
  253.0 4.4 %collective-permute-start.8 = (f32[1,16,256]{2,1,0:T(8,128)S(1)}, f32[1,16,256]{2,1,0:T(8,128)S(1)}, u32[]{:S(2)}, u32[]{:S(2)}) collective-permute-start(f32[1,16,256]{2,1,0:T(8,128)S(1)} %get-tuple-element.45), channel_id=1, source_target_pairs={{0,32},{32,64},{64,96},{96,128},{128,160},{160,192},{192,224},{1,3... | collective-permute-start | bytes 49160 | tf_op jit(solution)/shard_map/ppermute | solution.py:193
  259.3 3.1 collective-permute-done.9
  266.5 3.1 collective-permute-done.11
  274.1 18.9 %shard_map.90 = f32[8,128]{1,0:T(8,128)} custom-call(f32[8,128]{1,0:T(8,128)} %iota.60.x_ref), custom_call_target="tpu_custom_call" | custom-call | tf_op jit(solution)/shard_map/pallas_call | solution.py:121
  295.0 4.5 %collective-permute-start.12 = (f32[1,16,256]{2,1,0:T(8,128)S(1)}, f32[1,16,256]{2,1,0:T(8,128)S(1)}, u32[]{:S(2)}, u32[]{:S(2)}) collective-permute-start(f32[1,16,256]{2,1,0:T(8,128)S(1)} %get-tuple-element.43), channel_id=1, source_target_pairs={{0,32},{32,64},{64,96},{96,128},{128,160},{160,192},{192,224},{1,3... | collective-permute-start | bytes 49160 | tf_op jit(solution)/shard_map/ppermute | solution.py:193
  301.5 3.1 collective-permute-done.13
  308.5 3.4 collective-permute-done.15
  316.3 18.7 %shard_map.91 = f32[8,128]{1,0:T(8,128)} custom-call(f32[8,128]{1,0:T(8,128)} %iota.61.x_ref), custom_call_target="tpu_custom_call" | custom-call | tf_op jit(solution)/shard_map/pallas_call | solution.py:121
  (110 shorter events, 74.9 us)
Async XLA Ops:
  0.0 7.9 %copy-start.3 = (s32[2,1,512]{2,1,0:T(1,128)S(1)}, s32[2,1,512]{2,1,0:T(1,128)}, u32[]{:S(2)}) copy-start(s32[2,1,512]{2,1,0:T(1,128)} %param.14) | copy-start | bytes 12292
  0.0 8.8 %copy-start.4 = (s32[2,1,1]{0,2,1:T(1,128)S(1)}, s32[2,1,1]{0,2,1:T(1,128)}, u32[]{:S(2)}) copy-start(s32[2,1,1]{0,2,1:T(1,128)} %param.15) | copy-start | bytes 28
  10.2 2.8 copy-start.1
  35.1 30.8 %copy-start.2 = (f32[2,32,2048]{2,1,0:T(8,128)S(1)}, f32[2,32,2048]{2,1,0:T(8,128)}, u32[]{:S(2)}) copy-start(f32[2,32,2048]{2,1,0:T(8,128)} %param.9) | copy-start | bytes 1572868
  86.9 3.1 copy-start
  165.9 8.1 %collective-permute-start = (f32[1,16,256]{2,1,0:T(8,128)S(1)}, f32[1,16,256]{2,1,0:T(8,128)S(1)}, u32[]{:S(2)}, u32[]{:S(2)}) collective-permute-start(f32[1,16,256]{2,1,0:T(8,128)S(1)} %get-tuple-element.49), channel_id=1, source_target_pairs={{0,32},{32,64},{64,96},{96,128},{128,160},{160,192},{192,224},{1,3... | collective-permute-start | bytes 49160 | tf_op jit(solution)/shard_map/ppermute | solution.py:193
  172.1 5.1 %collective-permute-start.1 = (f32[1,16,256]{2,1,0:T(8,128)S(1)}, f32[1,16,256]{2,1,0:T(8,128)S(1)}, u32[]{:S(2)}, u32[]{:S(2)}) collective-permute-start(f32[1,16,256]{2,1,0:T(8,128)S(1)} %get-tuple-element.50), channel_id=1, source_target_pairs={{32,0},{64,32},{96,64},{128,96},{160,128},{192,160},{224,192},{33,... | collective-permute-start | bytes 49160 | tf_op jit(solution)/shard_map/ppermute | solution.py:195
  177.2 4.5 %collective-permute-start.2 = (f32[34,1,256]{2,1,0:T(1,128)S(1)}, f32[34,1,256]{2,1,0:T(1,128)S(1)}, u32[]{:S(2)}, u32[]{:S(2)}) collective-permute-start(f32[34,1,256]{2,1,0:T(1,128)S(1)} %get-tuple-element.41), channel_id=1, source_target_pairs={{0,1},{1,2},{2,3},{3,4},{4,5},{5,6},{6,7},{7,8},{8,9},{9,10},{10,1... | collective-permute-start | bytes 104456 | tf_op jit(solution)/shard_map/ppermute | solution.py:193
  179.7 4.7 %collective-permute-start.3 = (f32[34,1,256]{2,1,0:T(1,128)S(1)}, f32[34,1,256]{2,1,0:T(1,128)S(1)}, u32[]{:S(2)}, u32[]{:S(2)}) collective-permute-start(f32[34,1,256]{2,1,0:T(1,128)S(1)} %get-tuple-element.42), channel_id=1, source_target_pairs={{1,0},{2,1},{3,2},{4,3},{5,4},{6,5},{7,6},{8,7},{9,8},{10,9},{11,1... | collective-permute-start | bytes 104456 | tf_op jit(solution)/shard_map/ppermute | solution.py:195
  211.9 5.9 %collective-permute-start.4 = (f32[1,16,256]{2,1,0:T(8,128)S(1)}, f32[1,16,256]{2,1,0:T(8,128)S(1)}, u32[]{:S(2)}, u32[]{:S(2)}) collective-permute-start(f32[1,16,256]{2,1,0:T(8,128)S(1)} %get-tuple-element.47), channel_id=1, source_target_pairs={{0,32},{32,64},{64,96},{96,128},{128,160},{160,192},{192,224},{1,3... | collective-permute-start | bytes 49160 | tf_op jit(solution)/shard_map/ppermute | solution.py:193
  215.9 5.1 %collective-permute-start.5 = (f32[1,16,256]{2,1,0:T(8,128)S(1)}, f32[1,16,256]{2,1,0:T(8,128)S(1)}, u32[]{:S(2)}, u32[]{:S(2)}) collective-permute-start(f32[1,16,256]{2,1,0:T(8,128)S(1)} %get-tuple-element.48), channel_id=1, source_target_pairs={{32,0},{64,32},{96,64},{128,96},{160,128},{192,160},{224,192},{33,... | collective-permute-start | bytes 49160 | tf_op jit(solution)/shard_map/ppermute | solution.py:195
  221.0 3.8 %collective-permute-start.6 = (f32[34,1,256]{2,1,0:T(1,128)S(1)}, f32[34,1,256]{2,1,0:T(1,128)S(1)}, u32[]{:S(2)}, u32[]{:S(2)}) collective-permute-start(f32[34,1,256]{2,1,0:T(1,128)S(1)} %get-tuple-element.39), channel_id=1, source_target_pairs={{0,1},{1,2},{2,3},{3,4},{4,5},{5,6},{6,7},{7,8},{8,9},{9,10},{10,1... | collective-permute-start | bytes 104456 | tf_op jit(solution)/shard_map/ppermute | solution.py:193
  223.5 4.7 %collective-permute-start.7 = (f32[34,1,256]{2,1,0:T(1,128)S(1)}, f32[34,1,256]{2,1,0:T(1,128)S(1)}, u32[]{:S(2)}, u32[]{:S(2)}) collective-permute-start(f32[34,1,256]{2,1,0:T(1,128)S(1)} %get-tuple-element.40), channel_id=1, source_target_pairs={{1,0},{2,1},{3,2},{4,3},{5,4},{6,5},{7,6},{8,7},{9,8},{10,9},{11,1... | collective-permute-start | bytes 104456 | tf_op jit(solution)/shard_map/ppermute | solution.py:195
  253.0 6.3 %collective-permute-start.8 = (f32[1,16,256]{2,1,0:T(8,128)S(1)}, f32[1,16,256]{2,1,0:T(8,128)S(1)}, u32[]{:S(2)}, u32[]{:S(2)}) collective-permute-start(f32[1,16,256]{2,1,0:T(8,128)S(1)} %get-tuple-element.45), channel_id=1, source_target_pairs={{0,32},{32,64},{64,96},{96,128},{128,160},{160,192},{192,224},{1,3... | collective-permute-start | bytes 49160 | tf_op jit(solution)/shard_map/ppermute | solution.py:193
  257.4 5.1 %collective-permute-start.9 = (f32[1,16,256]{2,1,0:T(8,128)S(1)}, f32[1,16,256]{2,1,0:T(8,128)S(1)}, u32[]{:S(2)}, u32[]{:S(2)}) collective-permute-start(f32[1,16,256]{2,1,0:T(8,128)S(1)} %get-tuple-element.46), channel_id=1, source_target_pairs={{32,0},{64,32},{96,64},{128,96},{160,128},{192,160},{224,192},{33,... | collective-permute-start | bytes 49160 | tf_op jit(solution)/shard_map/ppermute | solution.py:195
  262.5 4.0 %collective-permute-start.10 = (f32[34,1,256]{2,1,0:T(1,128)S(1)}, f32[34,1,256]{2,1,0:T(1,128)S(1)}, u32[]{:S(2)}, u32[]{:S(2)}) collective-permute-start(f32[34,1,256]{2,1,0:T(1,128)S(1)} %get-tuple-element.37), channel_id=1, source_target_pairs={{0,1},{1,2},{2,3},{3,4},{4,5},{5,6},{6,7},{7,8},{8,9},{9,10},{10,1... | collective-permute-start | bytes 104456 | tf_op jit(solution)/shard_map/ppermute | solution.py:193
  264.9 4.7 %collective-permute-start.11 = (f32[34,1,256]{2,1,0:T(1,128)S(1)}, f32[34,1,256]{2,1,0:T(1,128)S(1)}, u32[]{:S(2)}, u32[]{:S(2)}) collective-permute-start(f32[34,1,256]{2,1,0:T(1,128)S(1)} %get-tuple-element.38), channel_id=1, source_target_pairs={{1,0},{2,1},{3,2},{4,3},{5,4},{6,5},{7,6},{8,7},{9,8},{10,9},{11,1... | collective-permute-start | bytes 104456 | tf_op jit(solution)/shard_map/ppermute | solution.py:195
  295.0 6.4 %collective-permute-start.12 = (f32[1,16,256]{2,1,0:T(8,128)S(1)}, f32[1,16,256]{2,1,0:T(8,128)S(1)}, u32[]{:S(2)}, u32[]{:S(2)}) collective-permute-start(f32[1,16,256]{2,1,0:T(8,128)S(1)} %get-tuple-element.43), channel_id=1, source_target_pairs={{0,32},{32,64},{64,96},{96,128},{128,160},{160,192},{192,224},{1,3... | collective-permute-start | bytes 49160 | tf_op jit(solution)/shard_map/ppermute | solution.py:193
  299.5 5.1 %collective-permute-start.13 = (f32[1,16,256]{2,1,0:T(8,128)S(1)}, f32[1,16,256]{2,1,0:T(8,128)S(1)}, u32[]{:S(2)}, u32[]{:S(2)}) collective-permute-start(f32[1,16,256]{2,1,0:T(8,128)S(1)} %get-tuple-element.44), channel_id=1, source_target_pairs={{32,0},{64,32},{96,64},{128,96},{160,128},{192,160},{224,192},{33,... | collective-permute-start | bytes 49160 | tf_op jit(solution)/shard_map/ppermute | solution.py:195
  304.7 3.8 %collective-permute-start.14 = (f32[34,1,256]{2,1,0:T(1,128)S(1)}, f32[34,1,256]{2,1,0:T(1,128)S(1)}, u32[]{:S(2)}, u32[]{:S(2)}) collective-permute-start(f32[34,1,256]{2,1,0:T(1,128)S(1)} %get-tuple-element.35), channel_id=1, source_target_pairs={{0,1},{1,2},{2,3},{3,4},{4,5},{5,6},{6,7},{7,8},{8,9},{9,10},{10,1... | collective-permute-start | bytes 104456 | tf_op jit(solution)/shard_map/ppermute | solution.py:193
  307.1 4.7 %collective-permute-start.15 = (f32[34,1,256]{2,1,0:T(1,128)S(1)}, f32[34,1,256]{2,1,0:T(1,128)S(1)}, u32[]{:S(2)}, u32[]{:S(2)}) collective-permute-start(f32[34,1,256]{2,1,0:T(1,128)S(1)} %get-tuple-element.36), channel_id=1, source_target_pairs={{1,0},{2,1},{3,2},{4,3},{5,4},{6,5},{7,6},{8,7},{9,8},{10,9},{11,1... | collective-permute-start | bytes 104456 | tf_op jit(solution)/shard_map/ppermute | solution.py:195

commit v3 on v2

--- a/solution.py
+++ b/solution.py
@@ -98,26 +98,30 @@
     total = x_ref[...]
     slot = 0
     for s, stage in enumerate(stages):
+        axis, stride, size = stage
+        position = lax.rem(lax.axis_index(axis) // stride, size)
         source = x_ref if s == 0 else buf.at[s - 1]
+        recv[slot] = total
         sends = []
-        for d, peer in enumerate(_stage_peers(stage)):
+        for d, peer in enumerate(_stage_peers(stage), start=1):
             copy = pltpu.make_async_remote_copy(
                 src_ref=source, dst_ref=recv.at[slot + d], send_sem=ssem.at[slot + d],
-                recv_sem=rsem.at[slot + d], device_id=_peer(stage[0], peer), device_id_type=MESH)
+                recv_sem=rsem.at[slot + d], device_id=_peer(axis, peer), device_id_type=MESH)
             copy.start()
             sends.append(copy)
         for copy in sends:
             copy.wait()
-        for d in range(len(sends)):
-            total = total + recv[slot + d]
-        slot += len(sends)
+        total = recv[slot + position]
+        for p in range(1, size):
+            total = total + recv[slot + lax.rem(position - p + size, size)]
+        slot += size
         if s + 1 < len(stages):
             buf[s] = total
     o_ref[...] = total
 
 
 def scalar_sum(x, stages):
-    slots = sum(size - 1 for _, _, size in stages)
+    slots = sum(size for _, _, size in stages)
     return pl.pallas_call(
         functools.partial(scalar_sum_kernel, stages),
         out_shape=jax.ShapeDtypeStruct(x.shape, x.dtype),
@@ -129,6 +133,7 @@
             pltpu.SemaphoreType.DMA((slots,)),
             pltpu.SemaphoreType.DMA((slots,)),
         ],
+        cost_estimate=pl.CostEstimate(flops=0, transcendentals=0, bytes_accessed=40_000_000),
         compiler_params=pltpu.CompilerParams(collective_id=2, has_side_effects=True),
     )(x)
 
@@ -182,21 +187,29 @@
     )(x, chosen, weights)
 
 
-def padded_2(cells, sides, width):
-    for axis, dim in sides:
-        count = lax.axis_size(axis)
-        ends = count - 1
-        head = lax.slice_in_dim(cells, 0, width, axis=dim)
-        tail = lax.slice_in_dim(cells, cells.shape[dim] - width, cells.shape[dim], axis=dim)
-        cells = jnp.concatenate(
-            [
-                lax.ppermute(tail, axis, [(i, (i + 1) % count) for i in range(ends)]),
-                cells,
-                lax.ppermute(head, axis, [((i + 1) % count, i) for i in range(ends)]),
-            ],
-            axis=dim,
-        )
-    return cells
+def shift_from(block, pairs_of):
+    count_z, count_x = lax.axis_size("gz"), lax.axis_size("gx")
+    pairs = []
+    for z in range(count_z):
+        for x in range(count_x):
+            target = pairs_of(z, x)
+            if 0 <= target[0] < count_z and 0 <= target[1] < count_x:
+                pairs.append((z * count_x + x, target[0] * count_x + target[1]))
+    return lax.ppermute(block, ("gz", "gx"), pairs)
+
+
+def padded_2(cells):
+    zero_line = jnp.zeros_like(cells[:1, :1])
+    low_z = shift_from(cells[-1:], lambda z, x: (z + 1, x))
+    high_z = shift_from(cells[:1], lambda z, x: (z - 1, x))
+    low_x = shift_from(cells[:, -1:], lambda z, x: (z, x + 1))
+    high_x = shift_from(cells[:, :1], lambda z, x: (z, x - 1))
+    low_z_high_x = shift_from(cells[-1:, :1], lambda z, x: (z + 1, x - 1))
+    high_z_low_x = shift_from(cells[:1, -1:], lambda z, x: (z - 1, x + 1))
+    top = jnp.concatenate([zero_line, low_z, low_z_high_x], axis=1)
+    middle = jnp.concatenate([low_x, cells, high_x], axis=1)
+    bottom = jnp.concatenate([high_z_low_x, high_z, zero_line], axis=1)
+    return jnp.concatenate([top, middle, bottom], axis=0)
 
 
 def tv_grad(padded):
@@ -276,12 +289,15 @@
     difference = art_volume - volume
     change_part = jnp.sum(difference * difference)
     stages = scalar_stages(lax.axis_size("gz"), lax.axis_size("gx"))
+    padded = padded_2(art_volume)
     smooth = art_volume
     change_total = None
     for sweep_index in range(TV_STEPS):
-        padded = padded_2(smooth, (("gz", 0), ("gx", 1)), 1)
         slope = tv_grad(pad_depth(padded))
         slope_part = jnp.sum(slope * slope)
+        more = sweep_index + 1 < TV_STEPS
+        if more:
+            slope_padded = padded_2(slope)
         if sweep_index == 0:
             totals = scalar_sum(pack_pair(slope_part, change_part), stages)
             change_total = totals[0, 1]
@@ -290,6 +306,8 @@
         slope_total = totals[0, 0]
         scale_now = step_gain * jnp.sqrt(change_total) / jnp.sqrt(slope_total + norm_floor)
         smooth = smooth - scale_now * slope
+        if more:
+            padded = padded - scale_now * slope_padded
     return smooth
 
 

time: 339 us -> 363 us (1.071); the launches traced: 338 us -> 357 us
  starting transfers between devices: 42.1 us -> 66.1 us
  waiting for transfers between devices: 25 us -> 3.81 us
  Pallas kernels: 205 us -> 215 us
  other arithmetic: 25.7 us -> 30.2 us
    ppermute x16 -> x24, starting transfers between devices: 42.1 us -> 66.1 us  [shift_from(): return lax.ppermute(block, ('gz', 'gx'), pairs)]
    ppermute x16 -> x24, waiting for transfers between devices: 25 us -> 3.81 us  [shift_from(): return lax.ppermute(block, ('gz', 'gx'), pairs)]
    pallas_call x4, Pallas kernels: 76.1 us -> 86.4 us  [scalar_sum(): pl.pallas_call(functools.partial(scalar_sum_kernel, stages), out_shape=ja...]
    mul x4, other arithmetic: 2.35 us -> 6.57 us  [tv_grad(): flow_z = diff_z * inverse]
  transfers between devices with their start and end apart: 16 -> 24, of which waited for: 8 -> 2; matrix products, arithmetic and copies ran while one was open for 0% -> 2% of each run, Pallas kernels for 0% -> 20%
where the time goes in v3:
time: 363 us; the launch traced here: 357 us
  Pallas kernels  215 us (59%)
  starting transfers between devices  66.1 us (18%)
  other arithmetic  30.2 us (8%)
  matrix products  19.5 us (5%)
  local copies, waits for them, and re-layouts  14.1 us (4%)
  between operations  8.26 us (2%)
  waiting for transfers between devices  3.81 us (1%)
    pallas_call x4, Pallas kernels, scalar_sum(): pl.pallas_call(functools.partial(scalar_sum_kernel, stages), out_shape=ja...  86.4 us
    pallas_call x4, Pallas kernels, block_apply(): pl.pallas_call(functools.partial(block_apply_kernel, transposed), out_sha...  77.4 us
    ppermute x24, starting transfers between devices, shift_from(): return lax.ppermute(block, ('gz', 'gx'), pairs)  66.1 us
    pallas_call x2, Pallas kernels, vector_sum(): pl.pallas_call(functools.partial(vector_sum_kernel, n), out_shape=jax.Sha...  51.7 us
  transfers between devices with their start and end apart: 24, of which 2 were waited for; matrix products, arithmetic and copies ran while one was open for 2% of the time, Pallas kernels for 20%

profile of v3, /device:TPU:1, one launch (start us, length us, event | category | flops | bytes accessed | tf_op | source)
XLA Modules:
  0.0 357.4 jit_solution(15873620054975827393)
XLA Ops:
  19.2 19.6 %shard_map.82 = f32[512,128]{1,0:T(8,128)} custom-call(bf16[512,128]{1,0:T(8,128)(2,1)} %fusion.20.x_ref, s32[512,1]{1,0:T(8,128)} %copy.11.blk_ref, bf16[64,128,128]{2,1,0:T(8,128)(2,1)} %w_ref.7), custom_call_target="tpu_custom_call" | custom-call | flops 1073741824 | bytes 2752512 | tf_op jit(solution)/shard_map/pallas_call | solution.py:179
  41.7 28.7 %shard_map.83 = bf16[32,16,256]{2,1,0:T(8,128)(2,1)} custom-call(bf16[32,16,256]{2,1,0:T(8,128)(2,1)} %pad_maximum_fusion.8.x_ref), custom_call_target="tpu_custom_call" | custom-call | tf_op jit(solution)/shard_map/pallas_call | solution.py:64
  73.7 19.2 %shard_map.84 = f32[512,128]{1,0:T(8,128)} custom-call(bf16[512,128]{1,0:T(8,128)(2,1)} %convolution_convert_fusion.2.x_ref, s32[512,1]{1,0:T(8,128)} %copy.11.blk_ref, bf16[64,128,128]{2,1,0:T(8,128)(2,1)} %w_ref.7), custom_call_target="tpu_custom_call" | custom-call | flops 1073741824 | bytes 2752512 | tf_op jit(solution)/shard_map/pallas_call | solution.py:179
  92.9 2.9 fusion.6
  97.4 19.2 %shard_map.85 = f32[512,128]{1,0:T(8,128)} custom-call(bf16[512,128]{1,0:T(8,128)(2,1)} %fusion.21.x_ref, s32[512,1]{1,0:T(8,128)} %copy.14.blk_ref, bf16[64,128,128]{2,1,0:T(8,128)(2,1)} %w_ref.7), custom_call_target="tpu_custom_call" | custom-call | flops 1073741824 | bytes 2752512 | tf_op jit(solution)/shard_map/pallas_call | solution.py:179
  119.4 22.9 %shard_map.86 = bf16[32,16,256]{2,1,0:T(8,128)(2,1)} custom-call(bf16[32,16,256]{2,1,0:T(8,128)(2,1)} %pad_maximum_fusion.9.x_ref), custom_call_target="tpu_custom_call" | custom-call | tf_op jit(solution)/shard_map/pallas_call | solution.py:64
  144.4 19.4 %shard_map.87 = f32[512,128]{1,0:T(8,128)} custom-call(bf16[512,128]{1,0:T(8,128)(2,1)} %convolution_convert_fusion.x_ref, s32[512,1]{1,0:T(8,128)} %copy.14.blk_ref, bf16[64,128,128]{2,1,0:T(8,128)(2,1)} %w_ref.7), custom_call_target="tpu_custom_call" | custom-call | flops 1073741824 | bytes 2752512 | tf_op jit(solution)/shard_map/pallas_call | solution.py:179
  163.8 2.9 fusion.7
  169.0 5.7 %collective-permute-start.4 = (f32[1,1,256]{2,1,0:T(1,128)S(1)}, f32[1,1,256]{2,1,0:T(1,128)S(1)}, u32[]{:S(2)}, u32[]{:S(2)}) collective-permute-start(f32[1,1,256]{2,1,0:T(1,128)S(1)} %get-tuple-element.56), channel_id=1, source_target_pairs={{32,1},{33,2},{34,3},{35,4},{36,5},{37,6},{38,7},{39,8},{40,9},{41... | collective-permute-start | bytes 3080 | tf_op jit(solution)/shard_map/ppermute | solution.py:198
  174.6 5.7 %collective-permute-start = (f32[1,16,256]{2,1,0:T(8,128)S(1)}, f32[1,16,256]{2,1,0:T(8,128)S(1)}, u32[]{:S(2)}, u32[]{:S(2)}) collective-permute-start(f32[1,16,256]{2,1,0:T(8,128)S(1)} %get-tuple-element.53), channel_id=1, source_target_pairs={{0,32},{1,33},{2,34},{3,35},{4,36},{5,37},{6,38},{7,39},{8,40},{9,... | collective-permute-start | bytes 49160 | tf_op jit(solution)/shard_map/ppermute | solution.py:198
  182.3 2.6 collective-permute-start.2
  186.9 2.7 collective-permute-done.3
  196.5 24.8 %shard_map.88 = f32[8,128]{1,0:T(8,128)} custom-call(f32[8,128]{1,0:T(8,128)} %broadcast_select_fusion.x_ref), custom_call_target="tpu_custom_call" | custom-call | bytes 40000000 | tf_op jit(solution)/shard_map/pallas_call | solution.py:125
  221.3 4.2 %collective-permute-start.10 = (f32[1,1,256]{2,1,0:T(1,128)S(1)}, f32[1,1,256]{2,1,0:T(1,128)S(1)}, u32[]{:S(2)}, u32[]{:S(2)}) collective-permute-start(f32[1,1,256]{2,1,0:T(1,128)S(1)} %get-tuple-element.50), channel_id=1, source_target_pairs={{32,1},{33,2},{34,3},{35,4},{36,5},{37,6},{38,7},{39,8},{40,9},{41... | collective-permute-start | bytes 3080 | tf_op jit(solution)/shard_map/ppermute | solution.py:198
  229.8 3.0 collective-permute-start.8
  243.8 4.3 %collective-permute-start.16 = (f32[1,1,256]{2,1,0:T(1,128)S(1)}, f32[1,1,256]{2,1,0:T(1,128)S(1)}, u32[]{:S(2)}, u32[]{:S(2)}) collective-permute-start(f32[1,1,256]{2,1,0:T(1,128)S(1)} %get-tuple-element.44), channel_id=1, source_target_pairs={{32,1},{33,2},{34,3},{35,4},{36,5},{37,6},{38,7},{39,8},{40,9},{41... | collective-permute-start | bytes 3080 | tf_op jit(solution)/shard_map/ppermute | solution.py:198
  248.1 5.0 %collective-permute-start.12 = (f32[1,16,256]{2,1,0:T(8,128)S(1)}, f32[1,16,256]{2,1,0:T(8,128)S(1)}, u32[]{:S(2)}, u32[]{:S(2)}) collective-permute-start(f32[1,16,256]{2,1,0:T(8,128)S(1)} %get-tuple-element.41), channel_id=1, source_target_pairs={{0,32},{1,33},{2,34},{3,35},{4,36},{5,37},{6,38},{7,39},{8,40},{9,... | collective-permute-start | bytes 49160 | tf_op jit(solution)/shard_map/ppermute | solution.py:198
  255.0 2.8 collective-permute-start.14
  260.5 24.6 %shard_map.89 = f32[8,128]{1,0:T(8,128)} custom-call(f32[8,128]{1,0:T(8,128)} %iota.59.x_ref), custom_call_target="tpu_custom_call" | custom-call | bytes 40000000 | tf_op jit(solution)/shard_map/pallas_call | solution.py:125
  292.7 4.7 %collective-permute-start.22 = (f32[1,1,256]{2,1,0:T(1,128)S(1)}, f32[1,1,256]{2,1,0:T(1,128)S(1)}, u32[]{:S(2)}, u32[]{:S(2)}) collective-permute-start(f32[1,1,256]{2,1,0:T(1,128)S(1)} %get-tuple-element.38), channel_id=1, source_target_pairs={{32,1},{33,2},{34,3},{35,4},{36,5},{37,6},{38,7},{39,8},{40,9},{41... | collective-permute-start | bytes 3080 | tf_op jit(solution)/shard_map/ppermute | solution.py:198
  297.4 4.7 %collective-permute-start.18 = (f32[1,16,256]{2,1,0:T(8,128)S(1)}, f32[1,16,256]{2,1,0:T(8,128)S(1)}, u32[]{:S(2)}, u32[]{:S(2)}) collective-permute-start(f32[1,16,256]{2,1,0:T(8,128)S(1)} %get-tuple-element.35), channel_id=1, source_target_pairs={{0,32},{1,33},{2,34},{3,35},{4,36},{5,37},{6,38},{7,39},{8,40},{9,... | collective-permute-start | bytes 49160 | tf_op jit(solution)/shard_map/ppermute | solution.py:198
  304.1 2.9 collective-permute-start.20
  309.6 20.6 %shard_map.90 = f32[8,128]{1,0:T(8,128)} custom-call(f32[8,128]{1,0:T(8,128)} %iota.60.x_ref), custom_call_target="tpu_custom_call" | custom-call | bytes 40000000 | tf_op jit(solution)/shard_map/pallas_call | solution.py:125
  337.7 16.4 %shard_map.91 = f32[8,128]{1,0:T(8,128)} custom-call(f32[8,128]{1,0:T(8,128)} %iota.61.x_ref), custom_call_target="tpu_custom_call" | custom-call | bytes 40000000 | tf_op jit(solution)/shard_map/pallas_call | solution.py:125
  (122 shorter events, 79.8 us)
Async XLA Ops:
  167.7 17.2 %collective-permute-start.1 = (f32[1,1,256]{2,1,0:T(1,128)S(1)}, f32[1,1,256]{2,1,0:T(1,128)S(1)}, u32[]{:S(2)}, u32[]{:S(2)}) collective-permute-start(f32[1,1,256]{2,1,0:T(1,128)S(1)} %get-tuple-element.55), channel_id=1, source_target_pairs={{1,32},{2,33},{3,34},{4,35},{5,36},{6,37},{7,38},{8,39},{9,40},{10... | collective-permute-start | bytes 3080 | tf_op jit(solution)/shard_map/ppermute | solution.py:198
  169.0 17.9 %collective-permute-start.4 = (f32[1,1,256]{2,1,0:T(1,128)S(1)}, f32[1,1,256]{2,1,0:T(1,128)S(1)}, u32[]{:S(2)}, u32[]{:S(2)}) collective-permute-start(f32[1,1,256]{2,1,0:T(1,128)S(1)} %get-tuple-element.56), channel_id=1, source_target_pairs={{32,1},{33,2},{34,3},{35,4},{36,5},{37,6},{38,7},{39,8},{40,9},{41... | collective-permute-start | bytes 3080 | tf_op jit(solution)/shard_map/ppermute | solution.py:198
  174.6 12.3 %collective-permute-start = (f32[1,16,256]{2,1,0:T(8,128)S(1)}, f32[1,16,256]{2,1,0:T(8,128)S(1)}, u32[]{:S(2)}, u32[]{:S(2)}) collective-permute-start(f32[1,16,256]{2,1,0:T(8,128)S(1)} %get-tuple-element.53), channel_id=1, source_target_pairs={{0,32},{1,33},{2,34},{3,35},{4,36},{5,37},{6,38},{7,39},{8,40},{9,... | collective-permute-start | bytes 49160 | tf_op jit(solution)/shard_map/ppermute | solution.py:198
  180.3 6.6 %collective-permute-start.5 = (f32[1,16,256]{2,1,0:T(8,128)S(1)}, f32[1,16,256]{2,1,0:T(8,128)S(1)}, u32[]{:S(2)}, u32[]{:S(2)}) collective-permute-start(f32[1,16,256]{2,1,0:T(8,128)S(1)} %get-tuple-element.54), channel_id=1, source_target_pairs={{32,0},{33,1},{34,2},{35,3},{36,4},{37,5},{38,6},{39,7},{40,8},{41... | collective-permute-start | bytes 49160 | tf_op jit(solution)/shard_map/ppermute | solution.py:198
  182.3 4.6 %collective-permute-start.2 = (f32[32,1,256]{2,1,0:T(1,128)S(1)}, f32[32,1,256]{2,1,0:T(1,128)S(1)}, u32[]{:S(2)}, u32[]{:S(2)}) collective-permute-start(f32[32,1,256]{2,1,0:T(1,128)S(1)} %get-tuple-element.57), channel_id=1, source_target_pairs={{0,1},{1,2},{2,3},{3,4},{4,5},{5,6},{6,7},{7,8},{8,9},{9,10},{10,1... | collective-permute-start | bytes 98312 | tf_op jit(solution)/shard_map/ppermute | solution.py:198
  184.9 4.7 %collective-permute-start.3 = (f32[32,1,256]{2,1,0:T(1,128)S(1)}, f32[32,1,256]{2,1,0:T(1,128)S(1)}, u32[]{:S(2)}, u32[]{:S(2)}) collective-permute-start(f32[32,1,256]{2,1,0:T(1,128)S(1)} %get-tuple-element.58), channel_id=1, source_target_pairs={{1,0},{2,1},{3,2},{4,3},{5,4},{6,5},{7,6},{8,7},{9,8},{10,9},{11,1... | collective-permute-start | bytes 98312 | tf_op jit(solution)/shard_map/ppermute | solution.py:198
  194.0 38.8 %collective-permute-start.7 = (f32[1,1,256]{2,1,0:T(1,128)S(1)}, f32[1,1,256]{2,1,0:T(1,128)S(1)}, u32[]{:S(2)}, u32[]{:S(2)}) collective-permute-start(f32[1,1,256]{2,1,0:T(1,128)S(1)} %get-tuple-element.49), channel_id=1, source_target_pairs={{1,32},{2,33},{3,34},{4,35},{5,36},{6,37},{7,38},{8,39},{9,40},{10... | collective-permute-start | bytes 3080 | tf_op jit(solution)/shard_map/ppermute | solution.py:198
  221.3 15.6 %collective-permute-start.10 = (f32[1,1,256]{2,1,0:T(1,128)S(1)}, f32[1,1,256]{2,1,0:T(1,128)S(1)}, u32[]{:S(2)}, u32[]{:S(2)}) collective-permute-start(f32[1,1,256]{2,1,0:T(1,128)S(1)} %get-tuple-element.50), channel_id=1, source_target_pairs={{32,1},{33,2},{34,3},{35,4},{36,5},{37,6},{38,7},{39,8},{40,9},{41... | collective-permute-start | bytes 3080 | tf_op jit(solution)/shard_map/ppermute | solution.py:198
  225.4 11.4 %collective-permute-start.6 = (f32[1,16,256]{2,1,0:T(8,128)S(1)}, f32[1,16,256]{2,1,0:T(8,128)S(1)}, u32[]{:S(2)}, u32[]{:S(2)}) collective-permute-start(f32[1,16,256]{2,1,0:T(8,128)S(1)} %get-tuple-element.47), channel_id=1, source_target_pairs={{0,32},{1,33},{2,34},{3,35},{4,36},{5,37},{6,38},{7,39},{8,40},{9,... | collective-permute-start | bytes 49160 | tf_op jit(solution)/shard_map/ppermute | solution.py:198
  227.4 9.5 %collective-permute-start.11 = (f32[1,16,256]{2,1,0:T(8,128)S(1)}, f32[1,16,256]{2,1,0:T(8,128)S(1)}, u32[]{:S(2)}, u32[]{:S(2)}) collective-permute-start(f32[1,16,256]{2,1,0:T(8,128)S(1)} %get-tuple-element.48), channel_id=1, source_target_pairs={{32,0},{33,1},{34,2},{35,3},{36,4},{37,5},{38,6},{39,7},{40,8},{41... | collective-permute-start | bytes 49160 | tf_op jit(solution)/shard_map/ppermute | solution.py:198
  229.8 7.1 %collective-permute-start.8 = (f32[32,1,256]{2,1,0:T(1,128)S(1)}, f32[32,1,256]{2,1,0:T(1,128)S(1)}, u32[]{:S(2)}, u32[]{:S(2)}) collective-permute-start(f32[32,1,256]{2,1,0:T(1,128)S(1)} %get-tuple-element.51), channel_id=1, source_target_pairs={{0,1},{1,2},{2,3},{3,4},{4,5},{5,6},{6,7},{7,8},{8,9},{9,10},{10,1... | collective-permute-start | bytes 98312 | tf_op jit(solution)/shard_map/ppermute | solution.py:198
  232.8 5.2 %collective-permute-start.9 = (f32[32,1,256]{2,1,0:T(1,128)S(1)}, f32[32,1,256]{2,1,0:T(1,128)S(1)}, u32[]{:S(2)}, u32[]{:S(2)}) collective-permute-start(f32[32,1,256]{2,1,0:T(1,128)S(1)} %get-tuple-element.52), channel_id=1, source_target_pairs={{1,0},{2,1},{3,2},{4,3},{5,4},{6,5},{7,6},{8,7},{9,8},{10,9},{11,1... | collective-permute-start | bytes 98312 | tf_op jit(solution)/shard_map/ppermute | solution.py:198
  242.5 15.3 %collective-permute-start.13 = (f32[1,1,256]{2,1,0:T(1,128)S(1)}, f32[1,1,256]{2,1,0:T(1,128)S(1)}, u32[]{:S(2)}, u32[]{:S(2)}) collective-permute-start(f32[1,1,256]{2,1,0:T(1,128)S(1)} %get-tuple-element.43), channel_id=1, source_target_pairs={{1,32},{2,33},{3,34},{4,35},{5,36},{6,37},{7,38},{8,39},{9,40},{10... | collective-permute-start | bytes 3080 | tf_op jit(solution)/shard_map/ppermute | solution.py:198
  243.8 43.2 %collective-permute-start.16 = (f32[1,1,256]{2,1,0:T(1,128)S(1)}, f32[1,1,256]{2,1,0:T(1,128)S(1)}, u32[]{:S(2)}, u32[]{:S(2)}) collective-permute-start(f32[1,1,256]{2,1,0:T(1,128)S(1)} %get-tuple-element.44), channel_id=1, source_target_pairs={{32,1},{33,2},{34,3},{35,4},{36,5},{37,6},{38,7},{39,8},{40,9},{41... | collective-permute-start | bytes 3080 | tf_op jit(solution)/shard_map/ppermute | solution.py:198
  248.1 38.9 %collective-permute-start.12 = (f32[1,16,256]{2,1,0:T(8,128)S(1)}, f32[1,16,256]{2,1,0:T(8,128)S(1)}, u32[]{:S(2)}, u32[]{:S(2)}) collective-permute-start(f32[1,16,256]{2,1,0:T(8,128)S(1)} %get-tuple-element.41), channel_id=1, source_target_pairs={{0,32},{1,33},{2,34},{3,35},{4,36},{5,37},{6,38},{7,39},{8,40},{9,... | collective-permute-start | bytes 49160 | tf_op jit(solution)/shard_map/ppermute | solution.py:198
  253.0 34.0 %collective-permute-start.17 = (f32[1,16,256]{2,1,0:T(8,128)S(1)}, f32[1,16,256]{2,1,0:T(8,128)S(1)}, u32[]{:S(2)}, u32[]{:S(2)}) collective-permute-start(f32[1,16,256]{2,1,0:T(8,128)S(1)} %get-tuple-element.42), channel_id=1, source_target_pairs={{32,0},{33,1},{34,2},{35,3},{36,4},{37,5},{38,6},{39,7},{40,8},{41... | collective-permute-start | bytes 49160 | tf_op jit(solution)/shard_map/ppermute | solution.py:198
  255.0 32.0 %collective-permute-start.14 = (f32[32,1,256]{2,1,0:T(1,128)S(1)}, f32[32,1,256]{2,1,0:T(1,128)S(1)}, u32[]{:S(2)}, u32[]{:S(2)}) collective-permute-start(f32[32,1,256]{2,1,0:T(1,128)S(1)} %get-tuple-element.45), channel_id=1, source_target_pairs={{0,1},{1,2},{2,3},{3,4},{4,5},{5,6},{6,7},{7,8},{8,9},{9,10},{10,1... | collective-permute-start | bytes 98312 | tf_op jit(solution)/shard_map/ppermute | solution.py:198
  257.8 29.3 %collective-permute-start.15 = (f32[32,1,256]{2,1,0:T(1,128)S(1)}, f32[32,1,256]{2,1,0:T(1,128)S(1)}, u32[]{:S(2)}, u32[]{:S(2)}) collective-permute-start(f32[32,1,256]{2,1,0:T(1,128)S(1)} %get-tuple-element.46), channel_id=1, source_target_pairs={{1,0},{2,1},{3,2},{4,3},{5,4},{6,5},{7,6},{8,7},{9,8},{10,9},{11,1... | collective-permute-start | bytes 98312 | tf_op jit(solution)/shard_map/ppermute | solution.py:198
  291.4 15.6 %collective-permute-start.19 = (f32[1,1,256]{2,1,0:T(1,128)S(1)}, f32[1,1,256]{2,1,0:T(1,128)S(1)}, u32[]{:S(2)}, u32[]{:S(2)}) collective-permute-start(f32[1,1,256]{2,1,0:T(1,128)S(1)} %get-tuple-element.37), channel_id=1, source_target_pairs={{1,32},{2,33},{3,34},{4,35},{5,36},{6,37},{7,38},{8,39},{9,40},{10... | collective-permute-start | bytes 3080 | tf_op jit(solution)/shard_map/ppermute | solution.py:198
  292.7 39.4 %collective-permute-start.22 = (f32[1,1,256]{2,1,0:T(1,128)S(1)}, f32[1,1,256]{2,1,0:T(1,128)S(1)}, u32[]{:S(2)}, u32[]{:S(2)}) collective-permute-start(f32[1,1,256]{2,1,0:T(1,128)S(1)} %get-tuple-element.38), channel_id=1, source_target_pairs={{32,1},{33,2},{34,3},{35,4},{36,5},{37,6},{38,7},{39,8},{40,9},{41... | collective-permute-start | bytes 3080 | tf_op jit(solution)/shard_map/ppermute | solution.py:198
  297.4 34.7 %collective-permute-start.18 = (f32[1,16,256]{2,1,0:T(8,128)S(1)}, f32[1,16,256]{2,1,0:T(8,128)S(1)}, u32[]{:S(2)}, u32[]{:S(2)}) collective-permute-start(f32[1,16,256]{2,1,0:T(8,128)S(1)} %get-tuple-element.35), channel_id=1, source_target_pairs={{0,32},{1,33},{2,34},{3,35},{4,36},{5,37},{6,38},{7,39},{8,40},{9,... | collective-permute-start | bytes 49160 | tf_op jit(solution)/shard_map/ppermute | solution.py:198
  302.1 30.0 %collective-permute-start.23 = (f32[1,16,256]{2,1,0:T(8,128)S(1)}, f32[1,16,256]{2,1,0:T(8,128)S(1)}, u32[]{:S(2)}, u32[]{:S(2)}) collective-permute-start(f32[1,16,256]{2,1,0:T(8,128)S(1)} %get-tuple-element.36), channel_id=1, source_target_pairs={{32,0},{33,1},{34,2},{35,3},{36,4},{37,5},{38,6},{39,7},{40,8},{41... | collective-permute-start | bytes 49160 | tf_op jit(solution)/shard_map/ppermute | solution.py:198
  304.1 28.1 %collective-permute-start.20 = (f32[32,1,256]{2,1,0:T(1,128)S(1)}, f32[32,1,256]{2,1,0:T(1,128)S(1)}, u32[]{:S(2)}, u32[]{:S(2)}) collective-permute-start(f32[32,1,256]{2,1,0:T(1,128)S(1)} %get-tuple-element.39), channel_id=1, source_target_pairs={{0,1},{1,2},{2,3},{3,4},{4,5},{5,6},{6,7},{7,8},{8,9},{9,10},{10,1... | collective-permute-start | bytes 98312 | tf_op jit(solution)/shard_map/ppermute | solution.py:198
  307.0 25.1 %collective-permute-start.21 = (f32[32,1,256]{2,1,0:T(1,128)S(1)}, f32[32,1,256]{2,1,0:T(1,128)S(1)}, u32[]{:S(2)}, u32[]{:S(2)}) collective-permute-start(f32[32,1,256]{2,1,0:T(1,128)S(1)} %get-tuple-element.40), channel_id=1, source_target_pairs={{1,0},{2,1},{3,2},{4,3},{5,4},{6,5},{7,6},{8,7},{9,8},{10,9},{11,1... | collective-permute-start | bytes 98312 | tf_op jit(solution)/shard_map/ppermute | solution.py:198
  (2 other events, 3.5 us)

commit v4 on v3

--- a/solution.py
+++ b/solution.py
@@ -138,6 +138,112 @@
     )(x)
 
 
+def halo_routes(depth, width):
+    count_z, count_x = lax.axis_size("gz"), lax.axis_size("gx")
+    z, x = lax.axis_index("gz"), lax.axis_index("gx")
+    up_z, down_z = lax.rem(z + 1, count_z), lax.rem(z + count_z - 1, count_z)
+    up_x, down_x = lax.rem(x + 1, count_x), lax.rem(x + count_x - 1, count_x)
+    return [
+        (0, depth, (up_z, x)),
+        (depth, depth, (down_z, x)),
+        (2 * depth, width, (z, up_x)),
+        (2 * depth + width, width, (z, down_x)),
+        (2 * depth + 2 * width, 1, (up_z, down_x)),
+        (2 * depth + 2 * width + 1, 1, (down_z, up_x)),
+    ]
+
+
+def tv_exchange_kernel(stages, shape, x_ref, f_ref, o_ref, h_ref, buf, recv, ssem, rsem, hrecv, hsend, hget):
+    routes = halo_routes(*shape)
+    barrier = pltpu.get_barrier_semaphore()
+    count = 0
+    for stage in stages:
+        for peer in _stage_peers(stage):
+            pl.semaphore_signal(barrier, inc=1, device_id=_peer(stage[0], peer), device_id_type=MESH)
+            count += 1
+    for _, _, target in routes:
+        pl.semaphore_signal(barrier, inc=1, device_id=target, device_id_type=MESH)
+        count += 1
+    pl.semaphore_wait(barrier, count)
+    halo = []
+    for k, (row, rows, target) in enumerate(routes):
+        copy = pltpu.make_async_remote_copy(
+            src_ref=f_ref.at[pl.ds(row, rows)], dst_ref=hrecv.at[pl.ds(row, rows)],
+            send_sem=hsend.at[k], recv_sem=hget.at[k], device_id=target, device_id_type=MESH)
+        copy.start()
+        halo.append(copy)
+    total = x_ref[...]
+    slot = 0
+    for s, stage in enumerate(stages):
+        axis, stride, size = stage
+        position = lax.rem(lax.axis_index(axis) // stride, size)
+        source = x_ref if s == 0 else buf.at[s - 1]
+        recv[slot] = total
+        sends = []
+        for d, peer in enumerate(_stage_peers(stage), start=1):
+            copy = pltpu.make_async_remote_copy(
+                src_ref=source, dst_ref=recv.at[slot + d], send_sem=ssem.at[slot + d],
+                recv_sem=rsem.at[slot + d], device_id=_peer(axis, peer), device_id_type=MESH)
+            copy.start()
+            sends.append(copy)
+        for copy in sends:
+            copy.wait()
+        total = recv[slot + position]
+        for p in range(1, size):
+            total = total + recv[slot + lax.rem(position - p + size, size)]
+        slot += size
+        if s + 1 < len(stages):
+            buf[s] = total
+    o_ref[...] = total
+    for copy in halo:
+        copy.wait()
+    h_ref[...] = hrecv[...]
+
+
+def tv_exchange(x, cells, stages):
+    faces = faces_of(cells)
+    slots = sum(size for _, _, size in stages)
+    return pl.pallas_call(
+        functools.partial(tv_exchange_kernel, stages, (cells.shape[1], cells.shape[0])),
+        out_shape=(jax.ShapeDtypeStruct(x.shape, x.dtype), jax.ShapeDtypeStruct(faces.shape, faces.dtype)),
+        in_specs=[pl.BlockSpec(memory_space=pltpu.VMEM)] * 2,
+        out_specs=(pl.BlockSpec(memory_space=pltpu.VMEM), pl.BlockSpec(memory_space=pltpu.VMEM)),
+        scratch_shapes=[
+            pltpu.VMEM((max(len(stages) - 1, 1),) + x.shape, x.dtype),
+            pltpu.VMEM((slots,) + x.shape, x.dtype),
+            pltpu.SemaphoreType.DMA((slots,)),
+            pltpu.SemaphoreType.DMA((slots,)),
+            pltpu.VMEM(faces.shape, faces.dtype),
+            pltpu.SemaphoreType.DMA((6,)),
+            pltpu.SemaphoreType.DMA((6,)),
+        ],
+        compiler_params=pltpu.CompilerParams(collective_id=3, has_side_effects=True),
+    )(x, faces)
+
+
+def faces_of(cells):
+    return jnp.concatenate(
+        [cells[-1], cells[0], cells[:, -1], cells[:, 0], cells[-1, :1], cells[0, -1:]], axis=0)
+
+
+def padded_from(cells, halo):
+    count_z, count_x = lax.axis_size("gz"), lax.axis_size("gx")
+    z, x = lax.axis_index("gz"), lax.axis_index("gx")
+    depth, width = cells.shape[1], cells.shape[0]
+    low_z = jnp.where(z > 0, halo[:depth], 0.0)[None]
+    high_z = jnp.where(z < count_z - 1, halo[depth:2 * depth], 0.0)[None]
+    low_x = jnp.where(x > 0, halo[2 * depth:2 * depth + width], 0.0)[:, None]
+    high_x = jnp.where(x < count_x - 1, halo[2 * depth + width:2 * depth + 2 * width], 0.0)[:, None]
+    corner = 2 * depth + 2 * width
+    low_z_high_x = jnp.where((z > 0) & (x < count_x - 1), halo[corner:corner + 1], 0.0)[None]
+    high_z_low_x = jnp.where((z < count_z - 1) & (x > 0), halo[corner + 1:corner + 2], 0.0)[None]
+    zero_line = jnp.zeros_like(cells[:1, :1])
+    top = jnp.concatenate([zero_line, low_z, low_z_high_x], axis=1)
+    middle = jnp.concatenate([low_x, cells, high_x], axis=1)
+    bottom = jnp.concatenate([high_z_low_x, high_z, zero_line], axis=1)
+    return jnp.concatenate([top, middle, bottom], axis=0)
+
+
 def scalar_stages(n_gz, n_gx):
     stages = [("gz", 1, n_gz)]
     if n_gx % 4 == 0 and n_gx > 4:
@@ -289,25 +395,19 @@
     difference = art_volume - volume
     change_part = jnp.sum(difference * difference)
     stages = scalar_stages(lax.axis_size("gz"), lax.axis_size("gx"))
-    padded = padded_2(art_volume)
+    totals, halo = tv_exchange(pack_pair(0.0, change_part), art_volume, stages)
+    change_total = totals[0, 1]
+    padded = padded_from(art_volume, halo)
     smooth = art_volume
-    change_total = None
     for sweep_index in range(TV_STEPS):
         slope = tv_grad(pad_depth(padded))
         slope_part = jnp.sum(slope * slope)
-        more = sweep_index + 1 < TV_STEPS
-        if more:
-            slope_padded = padded_2(slope)
-        if sweep_index == 0:
-            totals = scalar_sum(pack_pair(slope_part, change_part), stages)
-            change_total = totals[0, 1]
-        else:
-            totals = scalar_sum(pack_pair(slope_part, 0.0), stages)
+        totals, halo = tv_exchange(pack_pair(slope_part, 0.0), slope, stages)
         slope_total = totals[0, 0]
         scale_now = step_gain * jnp.sqrt(change_total) / jnp.sqrt(slope_total + norm_floor)
         smooth = smooth - scale_now * slope
-        if more:
-            padded = padded - scale_now * slope_padded
+        if sweep_index + 1 < TV_STEPS:
+            padded = padded - scale_now * padded_from(slope, halo)
     return smooth
 
 

time: 363 us -> 320 us (0.88)
  starting transfers between devices: 66.1 us -> 0 us
  local copies, waits for them, and re-layouts: 14.1 us -> 32.5 us
  other arithmetic: 30.2 us -> 38.5 us
  waiting for transfers between devices: 3.81 us -> 0 us
    ppermute x24 -> x0, starting transfers between devices: 66.1 us -> none  [shift_from(): return lax.ppermute(block, ('gz', 'gx'), pairs)]
    concatenate x0 -> x13, local copies, waits for them, and re-layouts: none -> 15.5 us  [the longest x5 15.3 us: faces_of(): jnp.concatenate([cells[-1], cells[0], cells[:, -1], cells[:, 0], cells[-1...]
    broadcast_in_dim x0 -> x12, other arithmetic: none -> 9.2 us  [the longest x4 3.12 us: padded_from(): low_x = jnp.where(x > 0, halo[2 * depth:2 * depth + width], 0.0)[:, None]]
    ppermute x24 -> x0, waiting for transfers between devices: 3.81 us -> none  [shift_from(): return lax.ppermute(block, ('gz', 'gx'), pairs)]
    pallas_call x4 -> x5, Pallas kernels: 86.4 us -> 86.6 us  [tv_exchange(): pl.pallas_call(functools.partial(tv_exchange_kernel, stages, (cells.shape...]
  transfers between devices with their start and end apart: 24 -> 0, of which waited for: 2 -> 0; matrix products, arithmetic and copies ran while one was open for 2% -> 0% of each run, Pallas kernels for 20% -> 0%
where the time goes in v4:
time: 320 us; the launch traced here: 314 us
  Pallas kernels  216 us (68%)
  other arithmetic  38.5 us (12%)
  local copies, waits for them, and re-layouts  32.5 us (10%)
  matrix products  19.4 us (6%)
  between operations  8.31 us (3%)
    pallas_call x5, Pallas kernels, tv_exchange(): pl.pallas_call(functools.partial(tv_exchange_kernel, stages, (cells.shape...  86.6 us
    pallas_call x4, Pallas kernels, block_apply(): pl.pallas_call(functools.partial(block_apply_kernel, transposed), out_sha...  77.4 us
    pallas_call x2, Pallas kernels, vector_sum(): pl.pallas_call(functools.partial(vector_sum_kernel, n), out_shape=jax.Sha...  51.7 us
    concatenate x5, local copies, waits for them, and re-layouts, faces_of(): jnp.concatenate([cells[-1], cells[0], cells[:, -1], cells[:, 0], cells[-1...  15.3 us

profile of v4, /device:TPU:1, one launch (start us, length us, event | category | flops | bytes accessed | tf_op | source)
XLA Modules:
  0.0 314.4 jit_solution(5412828663028583216)
XLA Ops:
  10.3 2.2 convert_reduce_fusion.1
  17.6 19.6 %shard_map.82 = f32[512,128]{1,0:T(8,128)} custom-call(bf16[512,128]{1,0:T(8,128)(2,1)} %fusion.8.x_ref, s32[512,1]{1,0:T(8,128)} %copy.36.blk_ref, bf16[64,128,128]{2,1,0:T(8,128)(2,1)} %w_ref.7), custom_call_target="tpu_custom_call" | custom-call | flops 1073741824 | bytes 2752512 | tf_op jit(solution)/shard_map/pallas_call | solution.py:285
  37.3 2.1 convolution_convert_fusion.3
  40.1 28.7 %shard_map.83 = bf16[32,16,256]{2,1,0:T(8,128)(2,1)} custom-call(bf16[32,16,256]{2,1,0:T(8,128)(2,1)} %pad_maximum_fusion.1.x_ref), custom_call_target="tpu_custom_call" | custom-call | tf_op jit(solution)/shard_map/pallas_call | solution.py:64
  74.0 19.2 %shard_map.84 = f32[512,128]{1,0:T(8,128)} custom-call(bf16[512,128]{1,0:T(8,128)(2,1)} %convolution_convert_fusion.2.x_ref, s32[512,1]{1,0:T(8,128)} %copy.36.blk_ref, bf16[64,128,128]{2,1,0:T(8,128)(2,1)} %w_ref.7), custom_call_target="tpu_custom_call" | custom-call | flops 1073741824 | bytes 2752512 | tf_op jit(solution)/shard_map/pallas_call | solution.py:285
  93.2 2.9 fusion.6
  98.3 19.2 %shard_map.85 = f32[512,128]{1,0:T(8,128)} custom-call(bf16[512,128]{1,0:T(8,128)(2,1)} %fusion.9.x_ref, s32[512,1]{1,0:T(8,128)} %copy.42.blk_ref, bf16[64,128,128]{2,1,0:T(8,128)(2,1)} %w_ref.7), custom_call_target="tpu_custom_call" | custom-call | flops 1073741824 | bytes 2752512 | tf_op jit(solution)/shard_map/pallas_call | solution.py:285
  117.5 2.1 convolution_convert_fusion.1
  120.3 22.9 %shard_map.86 = bf16[32,16,256]{2,1,0:T(8,128)(2,1)} custom-call(bf16[32,16,256]{2,1,0:T(8,128)(2,1)} %pad_maximum_fusion.2.x_ref), custom_call_target="tpu_custom_call" | custom-call | tf_op jit(solution)/shard_map/pallas_call | solution.py:64
  145.3 19.4 %shard_map.87 = f32[512,128]{1,0:T(8,128)} custom-call(bf16[512,128]{1,0:T(8,128)(2,1)} %convolution_convert_fusion.x_ref, s32[512,1]{1,0:T(8,128)} %copy.42.blk_ref, bf16[64,128,128]{2,1,0:T(8,128)(2,1)} %w_ref.7), custom_call_target="tpu_custom_call" | custom-call | flops 1073741824 | bytes 2752512 | tf_op jit(solution)/shard_map/pallas_call | solution.py:285
  164.7 2.9 fusion.7
  170.6 3.1 concatenate.81.f_ref
  173.6 19.7 %shard_map.88 = (f32[8,128]{1,0:T(8,128)}, f32[98,256]{1,0:T(8,128)}) custom-call(f32[8,128]{1,0:T(8,128)} %broadcast_select_fusion.x_ref, f32[98,256]{1,0:T(8,128)} %concatenate.81.f_ref), custom_call_target="tpu_custom_call" | custom-call | tf_op jit(solution)/shard_map/pallas_call | solution.py:206
  200.0 1.5 multiply_reduce_fusion.3
  202.8 3.1 concatenate.86.f_ref
  205.9 16.6 %shard_map.89 = (f32[8,128]{1,0:T(8,128)}, f32[98,256]{1,0:T(8,128)}) custom-call(f32[8,128]{1,0:T(8,128)} %iota.65.x_ref, f32[98,256]{1,0:T(8,128)} %concatenate.86.f_ref), custom_call_target="tpu_custom_call" | custom-call | tf_op jit(solution)/shard_map/pallas_call | solution.py:206
  229.3 1.5 multiply_reduce_fusion.2
  232.1 3.1 concatenate.91.f_ref
  235.2 16.9 %shard_map.90 = (f32[8,128]{1,0:T(8,128)}, f32[98,256]{1,0:T(8,128)}) custom-call(f32[8,128]{1,0:T(8,128)} %iota.66.x_ref, f32[98,256]{1,0:T(8,128)} %concatenate.91.f_ref), custom_call_target="tpu_custom_call" | custom-call | tf_op jit(solution)/shard_map/pallas_call | solution.py:206
  259.0 1.5 multiply_reduce_fusion.1
  261.9 3.1 concatenate.96.f_ref
  264.9 16.7 %shard_map.91 = (f32[8,128]{1,0:T(8,128)}, f32[98,256]{1,0:T(8,128)}) custom-call(f32[8,128]{1,0:T(8,128)} %iota.67.x_ref, f32[98,256]{1,0:T(8,128)} %concatenate.96.f_ref), custom_call_target="tpu_custom_call" | custom-call | tf_op jit(solution)/shard_map/pallas_call | solution.py:206
  291.2 3.1 concatenate.101.f_ref
  294.2 16.7 %shard_map.92 = (f32[8,128]{1,0:T(8,128)}, f32[98,256]{1,0:T(8,128)}) custom-call(f32[8,128]{1,0:T(8,128)} %iota.68.x_ref, f32[98,256]{1,0:T(8,128)} %concatenate.101.f_ref), custom_call_target="tpu_custom_call" | custom-call | tf_op jit(solution)/shard_map/pallas_call | solution.py:206
  (123 shorter events, 58.4 us)
Async XLA Ops:
  14.2 2.1 copy-start
  71.3 1.5 copy-start.1
